TPU v7x, 32 devices: a whole 2x2x4 slice. The times are simulated.
32 devices in a mesh: dp: 8 (over y, x, core), fsdp: 4 (over z).
Axes of the slice: x: 2, y: 2, z: 4, core: 2. Of those that a mesh axis runs over, the one named last changes fastest.
Arguments:
- frames: bfloat16 [2, 16384, 1024], P(None, ('dp', 'fsdp')), may hold values from -6 to 6
- lengths: int32 [2, 32, 16], P(None, ('dp', 'fsdp')), may hold values from 1 to 256, 512 in all within a row
- cotangent: bfloat16 [2, 16384, 1024], P(None, ('dp', 'fsdp')), may hold values from -6 to 6
- first_gain: bfloat16 [1024], P(('dp', 'fsdp')), may hold values from 0.099609375 to 1.8984375
- qkv_weight: bfloat16 [1024, 3072], P(('dp', 'fsdp')), may hold values from -0.1875 to 0.1875
- out_weight: bfloat16 [1024, 1024], P(('dp', 'fsdp')), may hold values from -0.5 to 0.5
- second_gain: bfloat16 [1024], P(('dp', 'fsdp')), may hold values from 0.099609375 to 1.8984375
- up_weight: bfloat16 [1024, 4096], P(('dp', 'fsdp')), may hold values from -0.1875 to 0.1875
- up_bias: bfloat16 [4096], P(('dp', 'fsdp')), may hold values from -3 to 3
- down_weight: bfloat16 [4096, 1024], P(('dp', 'fsdp')), may hold values from -0.09375 to 0.09375
- down_bias: bfloat16 [1024], P(('dp', 'fsdp')), may hold values from -3 to 3
Outputs:
- outputs: bfloat16 [2, 16384, 1024], P(None, ('dp', 'fsdp'))
- frames_grad: float32 [2, 16384, 1024], P(None, ('dp', 'fsdp'))
- first_gain_grad: float32 [1024], P(('dp', 'fsdp'))
- qkv_weight_grad: float32 [1024, 3072], P(('dp', 'fsdp'))
- out_weight_grad: float32 [1024, 1024], P(('dp', 'fsdp'))
- second_gain_grad: float32 [1024], P(('dp', 'fsdp'))
- up_weight_grad: float32 [1024, 4096], P(('dp', 'fsdp'))
- up_bias_grad: float32 [4096], P(('dp', 'fsdp'))
- down_weight_grad: float32 [4096, 1024], P(('dp', 'fsdp'))
- down_bias_grad: float32 [1024], P(('dp', 'fsdp'))
Inputs may be any that keep to these rules, and one draw needn't show every extreme that they name: In every row the 16 lengths sum to 512, and the longest is exactly 256; each entry is one item, placed in the row's micro-batch and on the row's device.
All inputs are finite; a program needn't handle non-finite values.
Results may differ from a plain program's by a relative error of at most 0.011.
Values may be sent and summed in bfloat16 or wider, within the bound.
A program may use at most 256 MiB of HBM per device.

v0:
```python
import jax
import jax.numpy as jnp
from jax import lax
from jax.sharding import PartitionSpec as P

D = 1024
HEADS = 16
HEAD_DIM = 64


EPS = 1e-06


def build_mask(span, length):
    ends = jnp.cumsum(span)
    position = jnp.arange(length, dtype=jnp.int32)
    segment = jnp.sum((position[:, None] >= ends[None, :]).astype(jnp.int32), axis=1)
    same = segment[:, None] == segment[None, :]
    return jnp.logical_and(same, position[:, None] >= position[None, :])


def normalize(x_val):
    factor = lax.rsqrt(jnp.mean(x_val * x_val, axis=-1, keepdims=True) + EPS)
    return (x_val * factor, factor)


def norm_back(normal, factor, gain, grad_out):
    gain_grad = jnp.sum(grad_out * normal, axis=0)
    scaled = grad_out * gain
    inner = jnp.mean(scaled * normal, axis=-1, keepdims=True)
    return (factor * (scaled - normal * inner), gain_grad)


def split_heads(project, count):
    queries = project[:, :D].reshape(count, HEADS, HEAD_DIM)
    key_rows = project[:, D : 2 * D].reshape(count, HEADS, HEAD_DIM)
    value_rows = project[:, 2 * D :].reshape(count, HEADS, HEAD_DIM)
    return (queries, key_rows, value_rows)


def masked_scores(queries, key_rows, mask):
    scores = (
        jnp.einsum("qhd,khd->hqk", queries, key_rows, preferred_element_type=jnp.float32) * 0.125
    )
    return jnp.where(mask[None], scores, -1e30)


def exact_gelu(value):
    return jax.nn.gelu(value, approximate=False)


def forward_pass(x_val, mask, params):
    first_gain, qkv_weight, out_weight, second_gain, up_weight, up_bias, down_weight, down_bias = (
        params
    )
    count = x_val.shape[0]
    normal_in, factor_in = normalize(x_val)
    entered = (normal_in * first_gain.astype(jnp.float32)).astype(jnp.bfloat16)
    project = jnp.dot(entered, qkv_weight, preferred_element_type=jnp.float32).astype(jnp.bfloat16)
    queries, key_rows, value_rows = split_heads(project, count)
    scores = masked_scores(queries, key_rows, mask)
    peak = jnp.max(scores, axis=-1, keepdims=True)
    expo = jnp.exp(scores - peak)
    total = jnp.sum(expo, axis=-1, keepdims=True)
    logsum = peak + jnp.log(total)
    attend = (expo / total).astype(jnp.bfloat16)
    attended = jnp.einsum("hqk,khd->qhd", attend, value_rows, preferred_element_type=jnp.float32)
    attended = attended.reshape(count, D).astype(jnp.bfloat16)
    middle = x_val + jnp.dot(attended, out_weight, preferred_element_type=jnp.float32)
    normal_mid, factor_mid = normalize(middle)
    second = (normal_mid * second_gain.astype(jnp.float32)).astype(jnp.bfloat16)
    hidden = jnp.dot(second, up_weight, preferred_element_type=jnp.float32) + up_bias.astype(
        jnp.float32
    )
    active = exact_gelu(hidden).astype(jnp.bfloat16)
    final = jnp.dot(active, down_weight, preferred_element_type=jnp.float32) + down_bias.astype(
        jnp.float32
    )
    kept = (
        normal_in,
        factor_in,
        entered,
        project,
        logsum,
        attended,
        normal_mid,
        factor_mid,
        second,
        hidden,
        active,
    )
    return (middle + final, kept)


def backward_pass(grad, mask, params, kept):
    first_gain, qkv_weight, out_weight, second_gain, up_weight, up_bias, down_weight, down_bias = (
        params
    )
    (
        normal_in,
        factor_in,
        entered,
        project,
        logsum,
        attended,
        normal_mid,
        factor_mid,
        second,
        hidden,
        active,
    ) = kept
    count = grad.shape[0]
    grad_final = grad.astype(jnp.bfloat16)
    down_bias_grad = jnp.sum(grad_final.astype(jnp.float32), axis=0)
    down_grad = jnp.einsum("rf,rd->fd", active, grad_final, preferred_element_type=jnp.float32)
    grad_active = jnp.einsum(
        "rd,fd->rf", grad_final, down_weight, preferred_element_type=jnp.float32
    )
    gelu_value, gelu_back = jax.vjp(exact_gelu, hidden)
    grad_hidden = gelu_back(grad_active)[0].astype(jnp.bfloat16)
    up_bias_grad = jnp.sum(grad_hidden.astype(jnp.float32), axis=0)
    up_grad = jnp.einsum("rd,rf->df", second, grad_hidden, preferred_element_type=jnp.float32)
    grad_second = jnp.einsum(
        "rf,df->rd", grad_hidden, up_weight, preferred_element_type=jnp.float32
    )
    grad_norm_mid, second_gain_grad = norm_back(
        normal_mid, factor_mid, second_gain.astype(jnp.float32), grad_second
    )
    grad_middle = grad + grad_norm_mid
    grad_branch = grad_middle.astype(jnp.bfloat16)
    out_grad = jnp.einsum("re,rd->ed", attended, grad_branch, preferred_element_type=jnp.float32)
    grad_attended = jnp.einsum(
        "rd,ed->re", grad_branch, out_weight, preferred_element_type=jnp.float32
    )
    grad_attended = grad_attended.astype(jnp.bfloat16).reshape(count, HEADS, HEAD_DIM)
    queries, key_rows, value_rows = split_heads(project, count)
    scores = masked_scores(queries, key_rows, mask)
    attend_full = jnp.exp(scores - logsum)
    attend = attend_full.astype(jnp.bfloat16)
    value_grad = jnp.einsum(
        "hqk,qhd->khd", attend, grad_attended, preferred_element_type=jnp.float32
    )
    grad_attend = jnp.einsum(
        "qhd,khd->hqk", grad_attended, value_rows, preferred_element_type=jnp.float32
    )
    row_total = jnp.sum(attend_full * grad_attend, axis=-1, keepdims=True)
    grad_scores = (attend_full * (grad_attend - row_total)).astype(jnp.bfloat16)
    query_grad = (
        jnp.einsum("hqk,khd->qhd", grad_scores, key_rows, preferred_element_type=jnp.float32)
        * 0.125
    )
    key_grad = (
        jnp.einsum("hqk,qhd->khd", grad_scores, queries, preferred_element_type=jnp.float32) * 0.125
    )
    grad_project = jnp.concatenate(
        (query_grad.reshape(count, D), key_grad.reshape(count, D), value_grad.reshape(count, D)),
        axis=1,
    )
    grad_project = grad_project.astype(jnp.bfloat16)
    qkv_grad = jnp.einsum("rd,re->de", entered, grad_project, preferred_element_type=jnp.float32)
    grad_entered = jnp.einsum(
        "re,de->rd", grad_project, qkv_weight, preferred_element_type=jnp.float32
    )
    grad_norm_in, first_gain_grad = norm_back(
        normal_in, factor_in, first_gain.astype(jnp.float32), grad_entered
    )
    frames_grad = grad_middle + grad_norm_in
    grads = (
        first_gain_grad,
        qkv_grad,
        out_grad,
        second_gain_grad,
        up_grad,
        up_bias_grad,
        down_grad,
        down_bias_grad,
    )
    return (frames_grad, grads)


def body(
    frames,
    lengths,
    cotangent,
    first_gain,
    qkv_weight,
    out_weight,
    second_gain,
    up_weight,
    up_bias,
    down_weight,
    down_bias,
):
    shards = (
        first_gain,
        qkv_weight,
        out_weight,
        second_gain,
        up_weight,
        up_bias,
        down_weight,
        down_bias,
    )
    owners = lax.axis_size(("dp", "fsdp"))
    totals = tuple(
        (jnp.zeros((piece.shape[0] * owners,) + piece.shape[1:], jnp.float32) for piece in shards)
    )
    out_list = []
    grad_list = []
    for batch in range(frames.shape[0]):
        gathered = (
            lax.all_gather(shards[0], ("dp", "fsdp"), axis=0, tiled=True),
            lax.all_gather(shards[1], ("dp", "fsdp"), axis=0, tiled=True),
            lax.all_gather(shards[2], ("dp", "fsdp"), axis=0, tiled=True),
            lax.all_gather(shards[3], ("dp", "fsdp"), axis=0, tiled=True),
            lax.all_gather(shards[4], ("dp", "fsdp"), axis=0, tiled=True),
            lax.all_gather(shards[5], ("dp", "fsdp"), axis=0, tiled=True),
            lax.all_gather(shards[6], ("dp", "fsdp"), axis=0, tiled=True),
            lax.all_gather(shards[7], ("dp", "fsdp"), axis=0, tiled=True),
        )
        mask = build_mask(lengths[batch, 0], frames.shape[1])
        output, kept = forward_pass(frames[batch].astype(jnp.float32), mask, gathered)
        out_list.append(output.astype(jnp.bfloat16))
        backward_params = (
            lax.all_gather(shards[0], ("dp", "fsdp"), axis=0, tiled=True),
            lax.all_gather(shards[1], ("dp", "fsdp"), axis=0, tiled=True),
            lax.all_gather(shards[2], ("dp", "fsdp"), axis=0, tiled=True),
            lax.all_gather(shards[3], ("dp", "fsdp"), axis=0, tiled=True),
            lax.all_gather(shards[4], ("dp", "fsdp"), axis=0, tiled=True),
            lax.all_gather(shards[5], ("dp", "fsdp"), axis=0, tiled=True),
            lax.all_gather(shards[6], ("dp", "fsdp"), axis=0, tiled=True),
            lax.all_gather(shards[7], ("dp", "fsdp"), axis=0, tiled=True),
        )
        frames_grad, grads = backward_pass(
            cotangent[batch].astype(jnp.float32), mask, backward_params, kept
        )
        grad_list.append(frames_grad)
        totals = tuple((running + local_part for running, local_part in zip(totals, grads)))
    totals = lax.psum_scatter(totals, ("dp", "fsdp"), scatter_dimension=0, tiled=True)
    outputs = jnp.stack(out_list, axis=0)
    frames_grad = jnp.stack(grad_list, axis=0)
    return (
        outputs,
        frames_grad,
        totals[0],
        totals[1],
        totals[2],
        totals[3],
        totals[4],
        totals[5],
        totals[6],
        totals[7],
    )


def solution(mesh):
    in_specs = (
        P(None, ("dp", "fsdp"), None),
        P(None, ("dp", "fsdp"), None),
        P(None, ("dp", "fsdp"), None),
        P(("dp", "fsdp")),
        P(("dp", "fsdp"), None),
        P(("dp", "fsdp"), None),
        P(("dp", "fsdp")),
        P(("dp", "fsdp"), None),
        P(("dp", "fsdp")),
        P(("dp", "fsdp"), None),
        P(("dp", "fsdp")),
    )
    out_specs = (
        P(None, ("dp", "fsdp"), None),
        P(None, ("dp", "fsdp"), None),
        P(("dp", "fsdp")),
        P(("dp", "fsdp"), None),
        P(("dp", "fsdp"), None),
        P(("dp", "fsdp")),
        P(("dp", "fsdp"), None),
        P(("dp", "fsdp")),
        P(("dp", "fsdp"), None),
        P(("dp", "fsdp")),
    )
    return jax.shard_map(body, mesh=mesh, in_specs=in_specs, out_specs=out_specs, check_vma=False)
```

profile of v0, /device:TPU:0, one launch (start us, length us, event | category | flops | bytes accessed | tf_op | source)
XLA Modules:
  0.0 1451.2 jit_solution(6699239157284963449)
XLA Ops:
  13.2 42.2 %all-reduce.8 = (bf16[1024]{0:T(1024)(128)(2,1)S(1)}, bf16[1024]{0:T(1024)(128)(2,1)S(1)}, bf16[1024]{0:T(1024)(128)(2,1)}) all-reduce(bf16[1024]{0:T(1024)(128)(2,1)S(1)} %dynamic-update-slice, bf16[1024]{0:T(1024)(128)(2,1)S(1)} %dynamic-update-slice.1, ...), channel_id=1, replica_groups=mesh['dp'=8,'fsdp'=4] {'dp','fsdp'}, use_global_device_ids=true, to_apply=%add | all-reduce | flops 3072 | bytes 12288
  58.1 66.3 %all-gather = bf16[32,1,128]{2,1,0:T(2,128)(2,1)S(1)} all-gather(bf16[1,1,128]{2,1,0:T(2,128)(2,1)} %bitcast.177), channel_id=1, replica_groups=mesh['dp'=8,'fsdp'=4] {'dp','fsdp'}, dimensions={0}, use_global_device_ids=true | all-gather | bytes 8448 | tf_op jit(solution)/shard_map/all_gather | solution.py:217
  125.6 6.8 convolution_convert_fusion
  136.0 2.7 copy.90
  140.9 6.6 convolution_convert_fusion.1
  156.1 10.0 fusion.99
  166.1 8.6 fusion
  175.3 8.5 fusion.49
  183.8 4.6 multiply_reduce_fusion.7
  188.4 9.1 fusion.98
  197.5 8.5 fusion.1
  206.6 7.9 fusion.48
  214.6 2.6 multiply_reduce_fusion.6
  217.2 3.6 all-gather.10.cloned.1.call-done
  220.7 7.8 fusion.93
  228.6 3.3 copy-done.59
  231.9 43.7 %multiply_convert_fusion.3 = (bf16[512,4096]{1,0:T(8,128)(2,1)}, f32[512,4096]{1,0:T(8,128)}, bf16[512,4096]{1,0:T(8,128)(2,1)}, f32[512,4096]{1,0:T(8,128)}, f32[512,4096]{1,0:T(8,128)}) fusion(f32[4096]{0:T(1024)S(1)} %bitcast.174, f32[512,4096]{1,0:T(8,128)S(1)} %fusion.93, bf16[1024,4096]{1,0:T(8,128)(2,1)S(1)} %copy-done.58, ...), kind=kOutput, calls=%fused_computation.41 | convolution fusion | flops 4573364224 | bytes 52451328 | tf_op jit(solution)/shard_map/dot_general | solution.py:72
  275.6 24.0 %all-gather.12.cloned.1.call-done = bf16[4096,1024]{1,0:T(8,128)(2,1)} async-done(((bf16[128,1024]{1,0:T(8,128)(2,1)}), bf16[4096,1024]{1,0:T(8,128)(2,1)}) %all-gather.12.cloned.1.call-update) | async-done | bytes 8388624 | tf_op jit(solution)/shard_map/all_gather | solution.py:218
  299.6 14.1 convert_reduce_fusion
  313.7 9.8 fusion.100
  323.6 15.9 %convert_reduce_fusion.1 = (f32[4096]{0:T(1024)}, bf16[512,4096]{1,0:T(8,128)(2,1)}) fusion(f32[512,4096]{1,0:T(8,128)} %get-tuple-element.32, bf16[4096,1024]{1,0:T(8,128)(2,1)} %all-gather.12.cloned.1.call-done, bf16[2,512,1024]{2,1,0:T(8,128)(2,1)S(1)} %copy-done.27, f32[512,4096]{1,0:T(8,128)} %get-tuple-element.61, f32[4096]{0:T(1024)S(1)} %bitcast.176), kind=kOutput, calls=%fused_computation.23 | convolution fusion | flops 4330614784 | bytes 30441472 | tf_op jit(solution)/shard_map/rd,fd->rf/dot_general | solution.py:116
  339.5 9.3 multiply_reduce_fusion.3
  348.8 3.0 convert_reduce_fusion.2
  351.8 3.3 fusion.80
  357.0 14.7 %multiply_reduce_fusion.1 = (f32[16,512]{1,0:T(8,128)}, f32[16,512,512]{1,2,0:T(8,128)}) fusion(f32[16,512,512]{1,2,0:T(8,128)} %get-tuple-element.56, f32[16,512]{1,0:T(8,128)} %log_add_fusion.1, bf16[512,16,64]{0,2,1:T(8,128)(2,1)S(1)} %bitcast.150, bf16[512,16,64]{0,2,1:T(8,128)(2,1)} %bitcast.164), kind=kOutput, calls=%fused_computation.4 | convolution fusion | flops 549445632 | bytes 35717120 | tf_op jit(solution)/shard_map/qhd,khd->hqk/dot_general | solution.py:143
  374.1 10.7 multiply_convert_fusion.1
  384.9 7.1 multiply_convert_fusion.6
  398.3 6.1 convolution_add_fusion.3
  404.5 14.4 multiply_reduce_fusion
  421.4 10.6 multiply_convert_fusion
  432.0 7.3 multiply_convert_fusion.4
  439.3 2.5 multiply_convert_fusion.5
  441.8 10.1 fusion.53
  451.9 4.6 fusion.50
  456.6 6.1 fusion.59
  462.7 9.9 convolution_add_fusion.2
  473.2 13.4 fusion.91
  486.6 12.2 convolution_add_fusion
  498.8 13.0 fusion.66
  511.8 12.0 convolution_add_fusion.1
  524.7 7.1 fusion.58
  531.8 9.3 fusion.38
  541.1 39.8 %all-reduce.7 = (f32[1024]{0:T(1024)S(1)}, f32[1024]{0:T(1024)S(1)}, f32[4096]{0:T(1024)S(1)}, f32[1024]{0:T(1024)S(1)}) all-reduce(f32[1024]{0:T(1024)S(1)} %add.160, f32[1024]{0:T(1024)S(1)} %add.163, f32[4096]{0:T(1024)S(1)} %add.165, f32[1024]{0:T(1024)S(1)} %add.167), channel_id=2, replica_groups=mesh['dp'=8,'fsdp'=4] {'dp','fsdp'}, use_global_device_ids=true, to_apply=%region_20.21.clone | all-reduce | flops 7168 | bytes 57344
  583.3 10.6 fusion.56
  593.9 8.5 fusion.57
  607.7 104.9 %reduce-scatter.5.cloned.1.call-done = f32[32,3072]{1,0:T(8,128)} async-done(((f32[1024,3072]{1,0:T(8,128)}), f32[32,3072]{1,0:T(8,128)}) %reduce-scatter.5.cloned.1.call-update) | async-done | bytes 393232 | tf_op jit(solution)/shard_map/reduce_scatter | solution.py:239
  712.6 366.3 %reduce-scatter.9.cloned.1.call-done = f32[32,4096]{1,0:T(8,128)} async-done(((f32[1024,4096]{1,0:T(8,128)}), f32[32,4096]{1,0:T(8,128)}) %reduce-scatter.9.cloned.1.call-update) | async-done | bytes 524304 | tf_op jit(solution)/shard_map/reduce_scatter | solution.py:239
  1078.9 365.2 %reduce-scatter.11.cloned.1.call-done = f32[128,1024]{1,0:T(8,128)} async-done(((f32[4096,1024]{1,0:T(8,128)}), f32[128,1024]{1,0:T(8,128)}) %reduce-scatter.11.cloned.1.call-update) | async-done | bytes 524304 | tf_op jit(solution)/shard_map/reduce_scatter | solution.py:239
  (219 shorter events, 47.6 us)
Async XLA Ops:
  7.2 118.5 %all-gather.6.cloned.1.call-start = ((), (), s32[]{:S(2)}) async-start(), calls=%async_computation.4 | async-start | bytes 6488064 | tf_op jit(solution)/shard_map/all_gather | solution.py:213
  7.9 175.9 %all-gather.8.cloned.1.call-start = ((), (), s32[]{:S(2)}) async-start(), calls=%async_computation.5 | async-start | bytes 2162688 | tf_op jit(solution)/shard_map/all_gather | solution.py:214
  8.7 212.1 %all-gather.10.cloned.1.call-start = ((), (), s32[]{:S(2)}) async-start(), calls=%async_computation.6 | async-start | bytes 8650752 | tf_op jit(solution)/shard_map/all_gather | solution.py:216
  9.4 290.2 %all-gather.12.cloned.1.call-start = ((), (), s32[]{:S(2)}) async-start(), calls=%async_computation.7 | async-start | bytes 8650752 | tf_op jit(solution)/shard_map/all_gather | solution.py:218
  10.0 597.7 %reduce-scatter.7.cloned.1.call-start = ((), (), s32[]{:S(2)}) async-start(), calls=%async_computation.9 | async-start | bytes 4325376 | tf_op jit(solution)/shard_map/reduce_scatter | solution.py:239
  55.4 85.5 %copy-start.41 = (f32[1024]{0:T(1024)}, f32[1024]{0:T(1024)S(1)}, u32[]{:S(2)}) copy-start(f32[1024]{0:T(1024)S(1)} %convert_element_type.142) | copy-start | bytes 12292
  125.6 15.3 %copy-start.53 = (f32[512]{0:T(512)}, f32[512]{0:T(512)S(1)}, u32[]{:S(2)}) copy-start(f32[512]{0:T(512)S(1)} %get-tuple-element.73) | copy-start | bytes 6148
  136.0 52.5 %copy-start.11 = (bf16[512,1024]{0,1:T(8,128)(2,1)}, bf16[512,1024]{0,1:T(8,128)(2,1)S(1)}, u32[]{:S(2)}) copy-start(bf16[512,1024]{0,1:T(8,128)(2,1)S(1)} %copy.91) | copy-start | bytes 3145732
  188.4 160.4 %copy-start.51 = (f32[512]{0:T(512)}, f32[512]{0:T(512)S(1)}, u32[]{:S(2)}) copy-start(f32[512]{0:T(512)S(1)} %add_rsqrt_fusion.2) | copy-start | bytes 6148
  217.2 11.4 copy-start.45
  220.7 11.1 copy-start.19
  220.7 11.1 copy-start.58
  313.7 9.8 copy-start.29
  313.7 9.8 copy-start.27
  323.6 15.9 %copy-start.4 = (f32[512,1024]{1,0:T(8,128)S(1)}, f32[512,1024]{1,0:T(8,128)}, u32[]{:S(2)}) copy-start(f32[512,1024]{1,0:T(8,128)} %get-tuple-element.60) | copy-start | bytes 6291460
  323.6 15.9 %copy-start.35 = (f32[512,1024]{1,0:T(8,128)S(1)}, f32[512,1024]{1,0:T(8,128)}, u32[]{:S(2)}) copy-start(f32[512,1024]{1,0:T(8,128)} %fusion.100) | copy-start | bytes 6291460
  323.6 15.9 %copy-start.46 = (f32[512]{0:T(512)S(1)}, f32[512]{0:T(512)}, u32[]{:S(2)}) copy-start(f32[512]{0:T(512)} %copy-done.45) | copy-start | bytes 6148
  357.0 14.7 %copy-start.16 = (bf16[512,1024]{0,1:T(8,128)(2,1)}, bf16[512,1024]{0,1:T(8,128)(2,1)S(1)}, u32[]{:S(2)}) copy-start(bf16[512,1024]{0,1:T(8,128)(2,1)S(1)} %copy.93) | copy-start | bytes 3145732
  357.0 14.7 %slice-start = ((s8[16777216]{0:T(1024)(128)(4,1)}), s8[4194304]{0:T(1024)(128)(4,1)S(1)}, s32[]{:S(2)}) async-start(s8[16777216]{0:T(1024)(128)(4,1)} %bitcast.136), calls=%async_computation.12 | async-start | bytes 8388608
  357.0 14.7 %slice-start.1 = ((s8[16777216]{0:T(1024)(128)(4,1)}), s8[4194304]{0:T(1024)(128)(4,1)S(1)}, s32[]{:S(2)}) async-start(s8[16777216]{0:T(1024)(128)(4,1)} %bitcast.136), calls=%async_computation.13 | async-start | bytes 8388608
  357.0 15.9 %slice-start.2 = ((s8[16777216]{0:T(1024)(128)(4,1)}), s8[4194304]{0:T(1024)(128)(4,1)S(1)}, s32[]{:S(2)}) async-start(s8[16777216]{0:T(1024)(128)(4,1)} %bitcast.136), calls=%async_computation.14 | async-start | bytes 8388608
  357.0 17.1 %slice-start.3 = ((s8[16777216]{0:T(1024)(128)(4,1)}), s8[4194304]{0:T(1024)(128)(4,1)S(1)}, s32[]{:S(2)}) async-start(s8[16777216]{0:T(1024)(128)(4,1)} %bitcast.136), calls=%async_computation.15 | async-start | bytes 8388608
  374.1 10.7 copy-start.15
  398.3 20.7 %copy-start.18 = (bf16[512,1024]{0,1:T(8,128)(2,1)}, bf16[512,1024]{0,1:T(8,128)(2,1)S(1)}, u32[]{:S(2)}) copy-start(bf16[512,1024]{0,1:T(8,128)(2,1)S(1)} %copy.97) | copy-start | bytes 3145732
  404.4 308.2 %reduce-scatter.5.cloned.1.call-start = ((), (), s32[]{:S(2)}) async-start(), calls=%async_computation.8 | async-start | bytes 12976128 | tf_op jit(solution)/shard_map/reduce_scatter | solution.py:239
  404.5 14.5 slice-start.8
  404.5 14.5 slice-start.9
  404.5 15.7 %slice-start.10 = ((s8[16777216]{0:T(1024)(128)(4,1)}), s8[4194304]{0:T(1024)(128)(4,1)S(1)}, s32[]{:S(2)}) async-start(s8[16777216]{0:T(1024)(128)(4,1)} %bitcast.140), calls=%async_computation.22 | async-start | bytes 8388608
  404.5 16.9 %slice-start.11 = ((s8[16777216]{0:T(1024)(128)(4,1)}), s8[4194304]{0:T(1024)(128)(4,1)S(1)}, s32[]{:S(2)}) async-start(s8[16777216]{0:T(1024)(128)(4,1)} %bitcast.140), calls=%async_computation.23 | async-start | bytes 8388608
  421.4 10.6 copy-start.14
  439.3 12.6 slice-start.4
  439.3 12.6 slice-start.5
  441.8 10.1 slice-start.6
  441.8 10.1 slice-start.7
  441.8 10.1 copy-start.17
  472.5 606.4 %reduce-scatter.9.cloned.1.call-start = ((), (), s32[]{:S(2)}) async-start(), calls=%async_computation.10 | async-start | bytes 17301504 | tf_op jit(solution)/shard_map/reduce_scatter | solution.py:239
  473.2 13.4 copy-start.5
  473.2 13.4 copy-start.30
  498.8 945.3 %reduce-scatter.11.cloned.1.call-start = ((), (), s32[]{:S(2)}) async-start(), calls=%async_computation.11 | async-start | bytes 17301504 | tf_op jit(solution)/shard_map/reduce_scatter | solution.py:239
  498.8 13.0 copy-start.23
  498.8 13.0 copy-start.28
  531.8 9.3 copy-start.36
  583.3 10.6 copy-start.6
  583.3 10.6 copy-start.24
  593.9 10.1 copy-start.8
  593.9 10.1 copy-start.10
  593.9 10.1 copy-start.37
  593.9 10.1 copy-start.38
  (32 other events, 148.0 us)
Sparse Core Ops, SparseCore 0:
  10.9 71.8 all-gather.5
  85.7 55.5 all-gather.7
  144.3 76.4 all-gather.9
  223.5 76.0 all-gather.11
  404.5 146.9 reduce-scatter.6
  558.0 154.5 reduce-scatter.4
  715.6 363.3 reduce-scatter.8
  1081.9 362.1 reduce-scatter.10
where the time goes:
time: 1460 us; the launch traced here: 1450 us
  waiting for transfers between devices  867 us (59%)
  matrix products  335 us (23%)
  blocking collectives  148 us (10%)
  other arithmetic  51.5 us (4%)
  local copies, waits for them, and re-layouts  34.5 us (2%)
  between operations  15.1 us (1%)
    reduce_scatter x4, waiting for transfers between devices, body(): lax.psum_scatter(totals, ('dp', 'fsdp'), scatter_dimension=0, tiled=True)  836 us
    unnamed x2, blocking collectives  82.1 us
    all_gather x1, blocking collectives, body(): lax.all_gather(shards[5], ('dp', 'fsdp'), axis=0, tiled=True)  66.3 us
    dot_general x2, matrix products, forward_pass(): jnp.dot(second, up_weight, preferred_element_type=jnp.float32)  51.5 us
    dot_general x2, matrix products, backward_pass(): jnp.einsum('rd,fd->rf', grad_final, down_weight, preferred_element_type=j...  30 us
  transfers between devices with their start and end apart: 8, of which 5 were waited for; matrix products, arithmetic and copies ran while one was open for 21% of the time, Pallas kernels for 0%

commit v1 on v0

v1 whole, which is shorter than its diff:
```python
import functools
import jax
import jax.numpy as jnp
from jax import lax
from jax.experimental import pallas as pl
from jax.experimental.pallas import tpu as pltpu
from jax.sharding import PartitionSpec as P

AXES = ("dp", "fsdp")
ROWS, WIDE, SKEW = 32, 512, 1


def bit_table(sizes):
    table = []
    for axis in AXES:
        stride = sizes[axis] // 2
        while stride:
            table.append((axis, stride))
            stride //= 2
    return table


def my_bits(table):
    where = {axis: lax.axis_index(axis) for axis in AXES}
    return [(where[axis] // stride) % 2 for axis, stride in table], where


def partner(table, bits, where, k):
    axis, stride = table[k]
    other = dict(where)
    other[axis] = where[axis] + stride * (1 - 2 * bits[k])
    return tuple(other[a] for a in AXES)


def greet(table, bits, where):
    barrier = pltpu.get_barrier_semaphore()
    for k in range(len(table)):
        pl.semaphore_signal(barrier, inc=1, device_id=partner(table, bits, where, k), device_id_type=pl.DeviceIdType.MESH)
    pl.semaphore_wait(barrier, len(table))


def orders(table):
    dp = [k for k, (axis, _) in enumerate(table) if axis == "dp"]
    rest = [k for k, (axis, _) in enumerate(table) if axis != "dp"]
    core, chips = dp[-1:], dp[:-1]
    return [core + chips + rest, core + chips[::-1] + rest]


def units_of(shapes):
    units = []
    for i, (rows, width) in enumerate(shapes):
        high, wide = min(rows, ROWS), min(width, WIDE)
        for r in range(0, rows, high):
            for c in range(0, width, 2 * wide):
                halves = [c] if c + wide >= width else [c, c + wide]
                units.append([(i, slice(r, r + high), slice(b, b + wide)) for b in halves])
    return units


def timetable(units, steps, skew):
    events, piece = [], 0
    for u, unit in enumerate(units):
        for h in range(len(unit)):
            events += [(u + skew * s, s, piece, h) for s in range(steps + 1)]
            piece += 1
    return [(p, s) for _, s, p, _ in sorted(events)]


def gather_kernel(table, n, chunks, times, *refs):
    shards, fulls = refs[:n], refs[n:2 * n]
    local_sem, send_sem, recv_sem = refs[2 * n:]
    bits, where = my_bits(table)
    steps = len(table)
    greet(table, bits, where)

    def view(c, done):
        i, rows, cols, _ = chunks[c]
        index = tuple(slice(None) if k in done else bits[k] for k in range(steps))
        return fulls[i].at[index + (rows, cols)]

    own, copies = [], {}
    for i in range(n):
        index = tuple(bits[k] for k in range(steps))
        copy = pltpu.make_async_copy(shards[i], fulls[i].at[index], local_sem.at[i])
        copy.start()
        own.append(copy)
    arrived = set()
    for c, s in times:
        i, rows, cols, order = chunks[c]
        if s > 0:
            copies[c, s - 1].wait_recv()
            if i not in arrived:
                arrived.add(i)
                own[i].wait()
        if s < steps:
            there = view(c, order[:s])
            copy = pltpu.make_async_remote_copy(
                src_ref=shards[i].at[rows, cols] if s == 0 else there, dst_ref=there,
                send_sem=send_sem.at[c, s], recv_sem=recv_sem.at[c, s],
                device_id=partner(table, bits, where, order[s]), device_id_type=pl.DeviceIdType.MESH)
            copy.start()
            copies[c, s] = copy
    for copy in copies.values():
        copy.wait_send()


def gather(shards, sizes, collective_id):
    table = bit_table(sizes)
    steps = len(table)
    two = [o[::-1] for o in orders(table)]
    units = units_of([a.shape for a in shards])
    chunks = [piece + (two[(h + u) % 2],) for u, unit in enumerate(units) for h, piece in enumerate(unit)]
    out = pl.pallas_call(
        functools.partial(gather_kernel, table, len(shards), chunks, timetable(units, steps, SKEW)),
        out_shape=[jax.ShapeDtypeStruct((2,) * steps + a.shape, a.dtype) for a in shards],
        in_specs=[pl.BlockSpec(memory_space=pl.ANY)] * len(shards),
        out_specs=[pl.BlockSpec(memory_space=pl.ANY)] * len(shards),
        scratch_shapes=[pltpu.SemaphoreType.DMA((len(shards),)), pltpu.SemaphoreType.DMA((len(chunks), steps)), pltpu.SemaphoreType.DMA((len(chunks), steps))],
        compiler_params=pltpu.CompilerParams(collective_id=collective_id, has_side_effects=True),
        name="gather",
    )(*shards)
    return [f.reshape((f.shape[-2] * 2 ** steps,) + f.shape[-1:]) for f in out]


def scatter_kernel(table, plan, *refs):
    n, chunks, times, steps = plan["n"], plan["chunks"], plan["times"], len(table)
    parts, outs = refs[:n], refs[n:2 * n]
    m = len(chunks)
    keep = refs[2 * n:2 * n + m]
    recv = [refs[2 * n + m + c * steps:2 * n + m + (c + 1) * steps] for c in range(m)]
    local_sem, send_sem, recv_sem = refs[2 * n + m + m * steps:]
    bits, where = my_bits(table)
    greet(table, bits, where)
    copies = {}
    loads = {}

    def index(order, s, last):
        out = []
        for k in range(steps):
            if k in order[1:s]:
                out.append(bits[k])
            elif k == order[0]:
                continue
            elif s < steps and k == order[s] and last is not None:
                out.append(last)
            else:
                out.append(slice(None))
        return tuple(out)

    def start(c, s):
        i, rows, cols, order = chunks[c]
        k = order[s]
        other = 1 - bits[k]
        if s == 0:
            full = tuple(other if q == k else slice(None) for q in range(steps))
            src = parts[i].at[full + (rows, cols)]
        else:
            src = keep[c].at[index(order, s, other)]
        copy = pltpu.make_async_remote_copy(
            src_ref=src, dst_ref=recv[c][s], send_sem=send_sem.at[c, s], recv_sem=recv_sem.at[c, s],
            device_id=partner(table, bits, where, k), device_id_type=pl.DeviceIdType.MESH)
        copy.start()
        copies[c, s] = copy

    def add(c, s):
        i, rows, cols, order = chunks[c]
        left = steps - s - 1
        if left == 0:
            own = keep[c][index(order, steps, None)] if steps > 1 else keep[c][...]
            outs[i][rows, cols] = own.astype(jnp.float32) + recv[c][s][...].astype(jnp.float32)
            return
        base = index(order, s, bits[order[s]] if s else None)

        @pl.loop(0, 2 ** left)
        def _(j):
            free, at = [], []
            for b in range(left):
                free.append((j // 2 ** (left - 1 - b)) % 2)
            pos = 0
            for e in base:
                if isinstance(e, slice):
                    at.append(free[pos])
                    pos += 1
                else:
                    at.append(e)
            here = tuple(at)
            got = recv[c][s][tuple(free)]
            keep[c][here] = (keep[c][here].astype(jnp.float32) + got.astype(jnp.float32)).astype(keep[c].dtype)

    for c, s in times:
        i, rows, cols, order = chunks[c]
        if s == 0:
            full = tuple(bits[k] if k == order[0] else slice(None) for k in range(steps))
            loads[c] = pltpu.make_async_copy(parts[i].at[full + (rows, cols)], keep[c], local_sem.at[c])
            loads[c].start()
        else:
            copies[c, s - 1].wait_recv()
            if s == 1:
                loads[c].wait()
            add(c, s - 1)
        if s < steps:
            start(c, s)
    for copy in copies.values():
        copy.wait_send()


def scatter(parts, sizes, collective_id):
    table = bit_table(sizes)
    steps = len(table)
    two = orders(table)
    owners = 2 ** steps
    parts = [a.reshape((2,) * steps + (a.shape[0] // owners, a.shape[1])) for a in parts]
    units = units_of([a.shape[-2:] for a in parts])
    chunks = [piece + (two[(h + u) % 2],) for u, unit in enumerate(units) for h, piece in enumerate(unit)]
    keep, recv = [], []
    for i, rows, cols, order in chunks:
        tail = (rows.stop - rows.start, cols.stop - cols.start)
        keep.append(pltpu.VMEM((2,) * (steps - 1) + tail, parts[i].dtype))
        recv += [pltpu.VMEM((2,) * (steps - 1 - s) + tail, parts[i].dtype) for s in range(steps)]
    plan = {"n": len(parts), "chunks": chunks, "times": timetable(units, steps, SKEW)}
    return pl.pallas_call(
        functools.partial(scatter_kernel, table, plan),
        out_shape=[jax.ShapeDtypeStruct(a.shape[-2:], jnp.float32) for a in parts],
        in_specs=[pl.BlockSpec(memory_space=pl.ANY)] * len(parts),
        out_specs=[pl.BlockSpec(memory_space=pltpu.VMEM)] * len(parts),
        scratch_shapes=keep + recv + [pltpu.SemaphoreType.DMA((len(chunks),)), pltpu.SemaphoreType.DMA((len(chunks), steps)), pltpu.SemaphoreType.DMA((len(chunks), steps))],
        compiler_params=pltpu.CompilerParams(collective_id=collective_id, has_side_effects=True, vmem_limit_bytes=56 * 2 ** 20),
        name="scatter",
    )(*parts)


D = 1024
HEADS = 16
HEAD_DIM = 64


EPS = 1e-06


def build_mask(span, length):
    slots = jnp.arange(span.shape[0], dtype=jnp.int32)
    ends = jnp.sum(jnp.where(slots[:, None] <= slots[None, :], span[:, None], 0), axis=0)
    position = jnp.arange(length, dtype=jnp.int32)
    segment = jnp.sum((position[:, None] >= ends[None, :]).astype(jnp.int32), axis=1)
    same = segment[:, None] == segment[None, :]
    return jnp.logical_and(same, position[:, None] >= position[None, :])


def normalize(x_val):
    factor = lax.rsqrt(jnp.mean(x_val * x_val, axis=-1, keepdims=True) + EPS)
    return (x_val * factor, factor)


def norm_back(normal, factor, gain, grad_out):
    gain_grad = jnp.sum(grad_out * normal, axis=0)
    scaled = grad_out * gain
    inner = jnp.mean(scaled * normal, axis=-1, keepdims=True)
    return (factor * (scaled - normal * inner), gain_grad)


def split_heads(project, count):
    queries = project[:, :D].reshape(count, -1, HEADS, HEAD_DIM)
    key_rows = project[:, D : 2 * D].reshape(count, -1, HEADS, HEAD_DIM)
    value_rows = project[:, 2 * D :].reshape(count, -1, HEADS, HEAD_DIM)
    return (queries, key_rows, value_rows)


def masked_scores(queries, key_rows, mask):
    scores = (
        jnp.einsum("bqhd,bkhd->bhqk", queries, key_rows, preferred_element_type=jnp.float32) * 0.125
    )
    return jnp.where(mask[:, None], scores, -1e30)


def exact_gelu(value):
    return jax.nn.gelu(value, approximate=False)


def forward_pass(x_val, mask, params):
    first_gain, qkv_weight, out_weight, second_gain, up_weight, up_bias, down_weight, down_bias = (
        params
    )
    count = x_val.shape[0]
    normal_in, factor_in = normalize(x_val)
    entered = (normal_in * first_gain.astype(jnp.float32)).astype(jnp.bfloat16)
    project = jnp.dot(entered, qkv_weight, preferred_element_type=jnp.float32).astype(jnp.bfloat16)
    queries, key_rows, value_rows = split_heads(project, mask.shape[0])
    scores = masked_scores(queries, key_rows, mask)
    peak = jnp.max(scores, axis=-1, keepdims=True)
    expo = jnp.exp(scores - peak)
    total = jnp.sum(expo, axis=-1, keepdims=True)
    logsum = peak + jnp.log(total)
    attend = (expo / total).astype(jnp.bfloat16)
    attended = jnp.einsum("bhqk,bkhd->bqhd", attend, value_rows, preferred_element_type=jnp.float32)
    attended = attended.reshape(count, D).astype(jnp.bfloat16)
    middle = x_val + jnp.dot(attended, out_weight, preferred_element_type=jnp.float32)
    normal_mid, factor_mid = normalize(middle)
    second = (normal_mid * second_gain.astype(jnp.float32)).astype(jnp.bfloat16)
    hidden = jnp.dot(second, up_weight, preferred_element_type=jnp.float32) + up_bias.astype(
        jnp.float32
    )
    active = exact_gelu(hidden).astype(jnp.bfloat16)
    final = jnp.dot(active, down_weight, preferred_element_type=jnp.float32) + down_bias.astype(
        jnp.float32
    )
    kept = (
        normal_in,
        factor_in,
        entered,
        project,
        logsum,
        attended,
        normal_mid,
        factor_mid,
        second,
        hidden,
        active,
    )
    return (middle + final, kept)


def backward_pass(grad, mask, params, kept):
    first_gain, qkv_weight, out_weight, second_gain, up_weight, up_bias, down_weight, down_bias = (
        params
    )
    (
        normal_in,
        factor_in,
        entered,
        project,
        logsum,
        attended,
        normal_mid,
        factor_mid,
        second,
        hidden,
        active,
    ) = kept
    count = grad.shape[0]
    grad_final = grad.astype(jnp.bfloat16)
    down_bias_grad = jnp.sum(grad_final.astype(jnp.float32), axis=0)
    down_grad = jnp.einsum("rf,rd->fd", active, grad_final, preferred_element_type=jnp.float32)
    grad_active = jnp.einsum(
        "rd,fd->rf", grad_final, down_weight, preferred_element_type=jnp.float32
    )
    gelu_value, gelu_back = jax.vjp(exact_gelu, hidden)
    grad_hidden = gelu_back(grad_active)[0].astype(jnp.bfloat16)
    up_bias_grad = jnp.sum(grad_hidden.astype(jnp.float32), axis=0)
    up_grad = jnp.einsum("rd,rf->df", second, grad_hidden, preferred_element_type=jnp.float32)
    grad_second = jnp.einsum(
        "rf,df->rd", grad_hidden, up_weight, preferred_element_type=jnp.float32
    )
    grad_norm_mid, second_gain_grad = norm_back(
        normal_mid, factor_mid, second_gain.astype(jnp.float32), grad_second
    )
    grad_middle = grad + grad_norm_mid
    grad_branch = grad_middle.astype(jnp.bfloat16)
    out_grad = jnp.einsum("re,rd->ed", attended, grad_branch, preferred_element_type=jnp.float32)
    grad_attended = jnp.einsum(
        "rd,ed->re", grad_branch, out_weight, preferred_element_type=jnp.float32
    )
    grad_attended = grad_attended.astype(jnp.bfloat16).reshape(mask.shape[0], -1, HEADS, HEAD_DIM)
    queries, key_rows, value_rows = split_heads(project, mask.shape[0])
    scores = masked_scores(queries, key_rows, mask)
    attend_full = jnp.exp(scores - logsum)
    attend = attend_full.astype(jnp.bfloat16)
    value_grad = jnp.einsum(
        "bhqk,bqhd->bkhd", attend, grad_attended, preferred_element_type=jnp.float32
    )
    grad_attend = jnp.einsum(
        "bqhd,bkhd->bhqk", grad_attended, value_rows, preferred_element_type=jnp.float32
    )
    row_total = jnp.sum(attend_full * grad_attend, axis=-1, keepdims=True)
    grad_scores = (attend_full * (grad_attend - row_total)).astype(jnp.bfloat16)
    query_grad = (
        jnp.einsum("bhqk,bkhd->bqhd", grad_scores, key_rows, preferred_element_type=jnp.float32)
        * 0.125
    )
    key_grad = (
        jnp.einsum("bhqk,bqhd->bkhd", grad_scores, queries, preferred_element_type=jnp.float32) * 0.125
    )
    grad_project = jnp.concatenate(
        (query_grad.reshape(count, D), key_grad.reshape(count, D), value_grad.reshape(count, D)),
        axis=1,
    )
    grad_project = grad_project.astype(jnp.bfloat16)
    qkv_grad = jnp.einsum("rd,re->de", entered, grad_project, preferred_element_type=jnp.float32)
    grad_entered = jnp.einsum(
        "re,de->rd", grad_project, qkv_weight, preferred_element_type=jnp.float32
    )
    grad_norm_in, first_gain_grad = norm_back(
        normal_in, factor_in, first_gain.astype(jnp.float32), grad_entered
    )
    frames_grad = grad_middle + grad_norm_in
    grads = (
        first_gain_grad,
        qkv_grad,
        out_grad,
        second_gain_grad,
        up_grad,
        up_bias_grad,
        down_grad,
        down_bias_grad,
    )
    return (frames_grad, grads)


def pack(vectors, owners, rows):
    flat = jnp.concatenate([v.reshape(owners, -1) for v in vectors], axis=1)
    return jnp.pad(flat, ((0, 0), (0, rows * 128 - flat.shape[1]))).reshape(owners * rows, 128)


def unpack(packed, owners, widths):
    flat = packed.reshape(owners, -1)
    out, at = [], 0
    for w in widths:
        out.append(flat[:, at:at + w].reshape(-1))
        at += w
    return out


def fits(sizes, shards):
    return all(s & (s - 1) == 0 for s in sizes.values()) and all(a.shape[0] % 16 == 0 for a in shards)


def body(sizes, frames, lengths, cotangent, *shards):
    owners = sizes["dp"] * sizes["fsdp"]
    weights = [shards[i] for i in (1, 2, 4, 6)]
    vectors = [shards[i] for i in (0, 3, 5, 7)]
    widths = [v.shape[0] for v in vectors]
    own_kernels = fits(sizes, weights)
    if own_kernels:
        packed, qkv, out, up, down = gather([pack(vectors, 1, 16)] + weights, sizes, 1)
        first, second, up_b, down_b = unpack(packed, owners, widths)
    else:
        qkv, out, up, down = [lax.all_gather(w, AXES, axis=0, tiled=True) for w in weights]
        first, second, up_b, down_b = [lax.all_gather(v, AXES, axis=0, tiled=True) for v in vectors]
    params = (first, qkv, out, second, up, up_b, down, down_b)
    batches, rows, width = frames.shape
    mask = jnp.stack([build_mask(lengths[b, 0], rows) for b in range(batches)])
    output, kept = forward_pass(frames.reshape(batches * rows, width).astype(jnp.float32), mask, params)
    frames_grad, grads = backward_pass(cotangent.reshape(batches * rows, width).astype(jnp.float32), mask, params, kept)
    big = [grads[i] for i in (1, 2, 4, 6)]
    small = [grads[i] for i in (0, 3, 5, 7)]
    if own_kernels:
        big = [g.astype(jnp.bfloat16) for g in (big[3], big[2], big[1], big[0])]
        down_g, up_g, out_g, qkv_g, packed = scatter(big + [pack(small, owners, 8)], sizes, 2)
        first_g, second_g, up_b_g, down_b_g = unpack(packed, 1, widths)
    else:
        qkv_g, out_g, up_g, down_g = [lax.psum_scatter(g.astype(jnp.float32), AXES, scatter_dimension=0, tiled=True) for g in big]
        first_g, second_g, up_b_g, down_b_g = [lax.psum_scatter(g, AXES, scatter_dimension=0, tiled=True) for g in small]
    shape = (batches, rows, width)
    return (output.astype(jnp.bfloat16).reshape(shape), frames_grad.reshape(shape), first_g, qkv_g, out_g, second_g, up_g, up_b_g, down_g, down_b_g)


def solution(mesh):
    in_specs = (
        P(None, ("dp", "fsdp"), None),
        P(None, ("dp", "fsdp"), None),
        P(None, ("dp", "fsdp"), None),
        P(("dp", "fsdp")),
        P(("dp", "fsdp"), None),
        P(("dp", "fsdp"), None),
        P(("dp", "fsdp")),
        P(("dp", "fsdp"), None),
        P(("dp", "fsdp")),
        P(("dp", "fsdp"), None),
        P(("dp", "fsdp")),
    )
    out_specs = (
        P(None, ("dp", "fsdp"), None),
        P(None, ("dp", "fsdp"), None),
        P(("dp", "fsdp")),
        P(("dp", "fsdp"), None),
        P(("dp", "fsdp"), None),
        P(("dp", "fsdp")),
        P(("dp", "fsdp"), None),
        P(("dp", "fsdp")),
        P(("dp", "fsdp"), None),
        P(("dp", "fsdp")),
    )
    return jax.shard_map(functools.partial(body, dict(mesh.shape)), mesh=mesh, in_specs=in_specs, out_specs=out_specs, check_vma=False)
```

time: 1460 us -> 649 us (0.44)
  waiting for transfers between devices: 867 us -> 0 us
  Pallas kernels: 0 us -> 257 us
  blocking collectives: 148 us -> 0 us
  matrix products: 335 us -> 258 us
  local copies, waits for them, and re-layouts: 34.5 us -> 74.6 us
    reduce_scatter x4 -> x0, waiting for transfers between devices: 836 us -> none  [body(): lax.psum_scatter(totals, ('dp', 'fsdp'), scatter_dimension=0, tiled=True)]
    pallas_call x0 -> x2, Pallas kernels: none -> 257 us  [the longest x1 130 us: gather(): pl.pallas_call(functools.partial(gather_kernel, table, len(shards), chunk...]
    unnamed x2 -> x0, blocking collectives: 82.1 us -> none
    all_gather x1 -> x0, blocking collectives: 66.3 us -> none  [body(): lax.all_gather(shards[5], ('dp', 'fsdp'), axis=0, tiled=True)]
    reshape x0 -> x13, local copies, waits for them, and re-layouts: none -> 44 us  [the longest x2 12.1 us: split_heads(): queries = project[:, :D].reshape(count, -1, HEADS, HEAD_DIM)]
    all_gather x4 -> x0, waiting for transfers between devices: 27.6 us -> none  [the longest x1 24 us: body(): lax.all_gather(shards[6], ('dp', 'fsdp'), axis=0, tiled=True)]
    dot_general x12 -> x6, matrix products: 98.6 us -> 88.1 us  [the longest x1 22.2 us: backward_pass(): jnp.einsum('bqhd,bkhd->bhqk', grad_attended, value_rows, preferred_elemen...]
    dot_general x2 -> x1, matrix products: 30 us -> 24 us  [backward_pass(): jnp.einsum('rd,fd->rf', grad_final, down_weight, preferred_element_type=j...]
  transfers between devices with their start and end apart: 8 -> 0, of which waited for: 5 -> 0; matrix products, arithmetic and copies ran while one was open for 21% -> 0% of each run, Pallas kernels for 0% -> 0%
where the time goes in v1:
time: 649 us; the launch traced here: 644 us
  matrix products  258 us (40%)
  Pallas kernels  257 us (40%)
  local copies, waits for them, and re-layouts  74.6 us (11%)
  other arithmetic  53.2 us (8%)
    pallas_call x1, Pallas kernels, gather(): pl.pallas_call(functools.partial(gather_kernel, table, len(shards), chunk...  130 us
    pallas_call x1, Pallas kernels, scatter(): pl.pallas_call(functools.partial(scatter_kernel, table, plan), out_shape=...  127 us
    dot_general x1, matrix products, forward_pass(): jnp.dot(second, up_weight, preferred_element_type=jnp.float32)  49.8 us
    convert_element_type x1, other arithmetic, backward_pass(): grad_scores = (attend_full * (grad_attend - row_total)).astype(jnp.bfloat16)  27.9 us
    dot_general x1, matrix products, backward_pass(): jnp.einsum('rd,fd->rf', grad_final, down_weight, preferred_element_type=j...  24 us
    dot_general x1, matrix products, backward_pass(): jnp.einsum('bqhd,bkhd->bhqk', grad_attended, value_rows, preferred_elemen...  22.2 us
    dot_general x1, matrix products, backward_pass(): jnp.einsum('rd,rf->df', second, grad_hidden, preferred_element_type=jnp.f...  16.4 us
    unnamed x67, local copies, waits for them, and re-layouts  15.7 us

profile of v1, /device:TPU:0, one launch (start us, length us, event | category | flops | bytes accessed | tf_op | source)
XLA Modules:
  0.0 644.2 jit_solution(5638842969648688894)
XLA Ops:
  1.7 1.4 fusion.42
  3.1 2.0 convert_reduce_fusion.1
  5.1 2.1 fusion.29
  8.9 130.3 %gather.1 = (bf16[2,2,2,2,2,16,128]{6,5,4,3,2,1,0:T(8,128)(2,1)}, bf16[2,2,2,2,2,32,3072]{6,5,4,3,2,1,0:T(8,128)(2,1)}, bf16[2,2,2,2,2,32,1024]{6,5,4,3,2,1,0:T(...) custom-call(bf16[16,128]{1,0:T(8,128)(2,1)} %bitcast.170, ...), custom_call_target="tpu_custom_call" | custom-call | tf_op jit(solution)/shard_map/gather/pallas_call | solution.py:113
  139.2 0.9 copy.93
  141.7 9.9 %convolution_convert_fusion.3 = bf16[1024,3072]{1,0:T(8,128)(2,1)S(1)} fusion(bf16[1024,1024]{1,0:T(8,128)(2,1)S(1)} %bitcast.165, bf16[1024,3072]{1,0:T(8,128)(2,1)} %bitcast.186), kind=kOutput, calls=%fused_computation.40 | convolution fusion | flops 6445596672 | bytes 14680064 | tf_op jit(solution)/shard_map/dot_general | solution.py:286
  151.6 2.7 fusion.46
  154.3 3.9 reshape.374
  158.2 4.5 copy.57
  162.7 6.6 %reshape.373 = bf16[2,512,16,64]{3,2,1,0:T(8,128)(2,1)} reshape(bf16[1024,1024]{1,0:T(8,128)(2,1)} %get-tuple-element.37) | data formatting | bytes 4194304 | tf_op jit(solution)/shard_map/reshape | solution.py:262
  169.3 5.4 copy.56
  174.8 6.3 reshape.372
  181.1 5.4 copy.58
  186.6 15.1 %fusion.47 = (f32[2,16,512]{2,1,0:T(8,128)S(1)}, f32[2,16,512,512]{2,3,1,0:T(8,128)}) fusion(bf16[2,512,16,64]{1,3,2,0:T(8,128)(2,1)} %copy.56, bf16[2,512,16,64]{1,3,2,0:T(8,128)(2,1)S(1)} %copy.57, pred[2,512,512]{1,2,0:T(8,128)(4,1)S(1)} %pad_add_fusion), kind=kOutput, calls=%fused_computation.119 | convolution fusion | flops 1098891264 | bytes 38338560 | tf_op jit(solution)/shard_map/bqhd,bkhd->bhqk/dot_general | solution.py:270
  201.6 13.3 %fusion = f32[2,16,512]{2,1,0:T(8,128)S(1)} fusion(f32[2,16,512,512]{2,3,1,0:T(8,128)} %get-tuple-element.51, f32[2,16,512]{2,1,0:T(8,128)S(1)} %get-tuple-element.50), kind=kLoop, calls=%fused_computation.6 | loop fusion | flops 16760832 | bytes 33685504 | tf_op jit(solution)/shard_map/reduce_sum | solution.py:291
  215.6 13.9 %convert_bitcast_fusion.1 = bf16[2,512,16,64]{1,3,2,0:T(8,128)(2,1)S(1)} fusion(bf16[2,512,16,64]{1,3,2,0:T(8,128)(2,1)S(1)} %copy-done.5, f32[2,16,512,512]{2,3,1,0:T(8,128)} %get-tuple-element.51, f32[2,16,512]{2,1,0:T(8,128)S(1)} %fusion, f32[2,16,512]{2,1,0:T(8,128)S(1)} %get-tuple-element.50), kind=kOutput, calls=%fused_computation.68 | convolution fusion | flops 1099956224 | bytes 37879808 | tf_op jit(solution)/shard_map/bhqk,bkhd->bqhd/dot_general | solution.py:294
  229.5 2.2 copy.60
  232.3 2.9 multiply_reduce_fusion.3
  235.8 49.8 %multiply_convert_fusion.1 = (bf16[1024,4096]{1,0:T(8,128)(2,1)}, f32[1024,4096]{1,0:T(8,128)}, f32[1024,4096]{1,0:T(8,128)}) fusion(f32[4096]{0:T(1024)S(1)} %fusion.41, bf16[1024,4096]{1,0:T(8,128)(2,1)S(1)} %bitcast.183, f32[1024,1024]{1,0:T(8,128)S(1)} %get-tuple-element.53, f32[1024]{0:T(1024)S(1)} %reshape.369, f32[1024]{0:T(1024)S(1)} %add_rsqrt_fusion), kind=kOutput, calls=%fused_computation.22 | convolution fusion | flops 8869904384 | bytes 54550528 | tf_op jit(solution)/shard_map/dot_general | solution.py:299
  285.7 24.0 %convert_reduce_fusion = (f32[4096]{0:T(1024)}, bf16[1024,4096]{1,0:T(8,128)(2,1)}) fusion(f32[1024,4096]{1,0:T(8,128)} %get-tuple-element.35, bf16[4096,1024]{1,0:T(8,128)(2,1)} %bitcast.184, bf16[1024,1024]{1,0:T(8,128)(2,1)S(1)} %bitcast.158, f32[1024,4096]{1,0:T(8,128)} %get-tuple-element.54, f32[4096]{0:T(1024)S(1)} %fusion.41), kind=kOutput, calls=%fused_computation.20 | convolution fusion | flops 8661233664 | bytes 52461568 | tf_op jit(solution)/shard_map/rd,fd->rf/dot_general | solution.py:343
  309.6 14.8 %add_convert_fusion = bf16[1024,1024]{1,0:T(8,128)(2,1)} fusion(f32[1024,1024]{1,0:T(8,128)S(1)} %get-tuple-element.53, f32[1024]{0:T(1024)S(1)} %copy-done.20, bf16[1024,4096]{1,0:T(8,128)(2,1)} %get-tuple-element.34, bf16[4096,1024]{1,0:T(8,128)(2,1)} %bitcast.185), kind=kOutput, calls=%fused_computation.64 | convolution fusion | flops 8593080320 | bytes 23072768 | tf_op jit(solution)/shard_map/dot_general | solution.py:303
  324.4 14.3 %multiply_reduce_fusion.1 = (f32[1024]{0:T(1024)S(1)}, f32[1024]{0:T(1024)S(1)}, f32[1024,1024]{1,0:T(8,128)S(1)}) fusion(f32[1024,1024]{1,0:T(8,128)S(1)} %get-tuple-element.53, f32[1024]{0:T(1024)S(1)} %add_rsqrt_fusion, f32[1024]{0:T(1024)S(1)} %reshape.369, bf16[1024,4096]{1,0:T(8,128)(2,1)} %get-tuple-element.60, bf16[1024,4096]{1,0:T(8,128)(2,1)} %bitcast.180), kind=kOutput, calls=%fused_computation.59 | convolution fusion | flops 8596224000 | bytes 25182208 | tf_op jit(solution)/shard_map/rf,df->rd/dot_general | solution.py:350
  338.8 14.6 %convolution_convert_fusion.1 = bf16[4096,1024]{1,0:T(8,128)(2,1)} fusion(bf16[1024,4096]{1,0:T(8,128)(2,1)} %get-tuple-element.34, bf16[1024,1024]{1,0:T(8,128)(2,1)S(1)} %bitcast.159), kind=kOutput, calls=%fused_computation.38 | convolution fusion | flops 8594128896 | bytes 18874368 | tf_op jit(solution)/shard_map/rf,rd->fd/dot_general | solution.py:342
  353.4 1.8 multiply_add_fusion
  355.2 16.4 %convolution_convert_fusion = bf16[1024,4096]{1,0:T(8,128)(2,1)} fusion(bf16[1024,4096]{1,0:T(8,128)(2,1)} %get-tuple-element.60, f32[1024,1024]{1,0:T(8,128)S(1)} %get-tuple-element.53, f32[1024]{0:T(1024)S(1)} %reshape.369, f32[1024]{0:T(1024)S(1)} %add_rsqrt_fusion), kind=kOutput, calls=%fused_computation.37 | convolution fusion | flops 8597274624 | bytes 20979712 | tf_op jit(solution)/shard_map/rd,rf->df/dot_general | solution.py:349
  371.6 3.6 convolution_convert_fusion.4
  375.3 2.4 convolution_convert_fusion.5
  377.8 4.0 reshape.375
  381.7 4.5 copy.62
  386.2 15.4 %convert_bitcast_fusion = bf16[2,512,16,64]{1,3,2,0:T(8,128)(2,1)} fusion(bf16[2,512,16,64]{1,3,2,0:T(8,128)(2,1)S(1)} %copy.62, f32[2,16,512,512]{2,3,1,0:T(8,128)} %get-tuple-element.51, f32[2,16,512]{2,1,0:T(8,128)S(1)} %copy-done.12), kind=kOutput, calls=%fused_computation.67 | convolution fusion | flops 1091567616 | bytes 37814272 | tf_op jit(solution)/shard_map/bhqk,bqhd->bkhd/dot_general | solution.py:367
  401.6 3.9 copy.72
  405.5 1.9 copy.90
  407.4 22.2 %multiply_reduce_fusion = (f32[2,16,512]{2,1,0:T(8,128)S(1)}, f32[2,16,512,512]{2,3,1,0:T(8,128)}) fusion(f32[2,16,512,512]{2,3,1,0:T(8,128)} %get-tuple-element.51, f32[2,16,512]{2,1,0:T(8,128)S(1)} %copy-done.12, bf16[2,512,16,64]{1,3,2,0:T(8,128)(2,1)S(1)} %copy.62, bf16[2,512,16,64]{1,3,2,0:T(8,128)(2,1)S(1)} %copy-done.6), kind=kOutput, calls=%fused_computation.1 | convolution fusion | flops 1098891264 | bytes 71434240 | tf_op jit(solution)/shard_map/bqhd,bkhd->bhqk/dot_general | solution.py:370
  429.6 27.9 %multiply_convert_fusion = bf16[2,16,512,512]{2,3,1,0:T(8,128)(2,1)} fusion(f32[2,16,512,512]{2,3,1,0:T(8,128)} %get-tuple-element.57, f32[2,16,512,512]{2,3,1,0:T(8,128)} %get-tuple-element.51, f32[2,16,512]{2,1,0:T(8,128)S(1)} %get-tuple-element.56, f32[2,16,512]{2,1,0:T(8,128)S(1)} %copy-done.12), kind=kLoop, calls=%fused_computation | loop fusion | flops 33554432 | bytes 84017152 | tf_op jit(solution)/shard_map/convert_element_type | solution.py:374
  457.5 13.0 %fusion.35 = bf16[2,512,16,64]{1,3,2,0:T(8,128)(2,1)} fusion(bf16[2,512,16,64]{1,3,2,0:T(8,128)(2,1)} %copy.56, bf16[2,16,512,512]{2,3,1,0:T(8,128)(2,1)} %multiply_convert_fusion), kind=kOutput, calls=%fused_computation.73 | convolution fusion | flops 1075838976 | bytes 20971520 | tf_op jit(solution)/shard_map/bhqk,bqhd->bkhd/dot_general | solution.py:380
  470.6 8.6 %fusion.34 = bf16[2,512,16,64]{1,3,2,0:T(8,128)(2,1)S(1)} fusion(bf16[2,512,16,64]{1,3,2,0:T(8,128)(2,1)S(1)} %copy-done.1, bf16[2,16,512,512]{2,3,1,0:T(8,128)(2,1)} %multiply_convert_fusion), kind=kOutput, calls=%fused_computation.72 | convolution fusion | flops 1075838976 | bytes 20971520 | tf_op jit(solution)/shard_map/bhqk,bkhd->bqhd/dot_general | solution.py:376
  479.1 2.2 copy.66
  481.9 2.2 copy.69
  486.9 8.2 %fusion.28 = (f32[1024]{0:T(1024)S(1)}, f32[1024]{0:T(1024)S(1)}, bf16[1024,1024]{1,0:T(8,128)(2,1)S(1)}, f32[1024,1024]{1,0:T(8,128)S(1)}) fusion(bf16[2,512,1024]{2,1,0:T(8,128)(2,1)S(1)} %copy-done.4, f32[1024]{0:T(1024)S(1)} %bitcast.172, f32[1024]{0:T(1024)S(1)} %copy-done.17, bf16[1024,3072]{0,1:T(8,128)(2,1)S(1)} %constant_dynamic-update-slice_fusion, ...), kind=kOutput, calls=%fused_computation.54 | convolution fusion | flops 6451886080 | bytes 20987904 | tf_op jit(solution)/shard_map/re,de->rd/dot_general | solution.py:388
  495.1 8.7 %convolution_convert_fusion.2 = bf16[1024,3072]{1,0:T(8,128)(2,1)} fusion(bf16[1024,1024]{1,0:T(8,128)(2,1)S(1)} %get-tuple-element.39, bf16[1024,3072]{0,1:T(8,128)(2,1)S(1)} %constant_dynamic-update-slice_fusion), kind=kOutput, calls=%fused_computation.39 | convolution fusion | flops 6445596672 | bytes 14680064 | tf_op jit(solution)/shard_map/rd,re->de/dot_general | solution.py:387
  503.8 2.7 fusion.26
  507.3 127.0 %scatter.1 = (f32[128,1024]{1,0:T(8,128)}, f32[32,4096]{1,0:T(8,128)}, f32[32,1024]{1,0:T(8,128)}, f32[32,3072]{1,0:T(8,128)}, f32[8,128]{1,0:T(8,128)}) custom-call(bf16[2,2,2,2,2,128,1024]{6,5,4,3,2,1,0:T(8,128)(2,1)} %bitcast.149, bf16[2,2,2,2,2,32,4096]{6,5,4,3,2,1,0:T(8,128)(2,1)} %bitcast.150, bf16[2,2,2,2,2,32,1024]{6,5,4,3,2,1,0:T(8,128)(2,1)} %bitcast.162, ...), custom_call_target="tpu_custom_call" | custom-call | tf_op jit(solution)/shard_map/scatter/pallas_call | solution.py:221
  634.3 1.2 slice_bitcast_fusion.2
  635.6 1.3 slice_bitcast_fusion.1
  636.8 1.8 copy.100
  638.6 1.6 copy.101
  640.2 1.9 copy.102
  642.0 1.9 copy.103
  (86 shorter events, 10.5 us)
Async XLA Ops:
  0.6 140.5 %copy-start.2 = (bf16[2,512,1024]{2,1,0:T(8,128)(2,1)S(1)}, bf16[2,512,1024]{2,1,0:T(8,128)(2,1)}, u32[]{:S(2)}) copy-start(bf16[2,512,1024]{2,1,0:T(8,128)(2,1)} %param.11) | copy-start | bytes 6291460
  140.5 11.1 %copy-start.16 = (f32[1024]{0:T(1024)}, f32[1024]{0:T(1024)S(1)}, u32[]{:S(2)}) copy-start(f32[1024]{0:T(1024)S(1)} %reshape.368) | copy-start | bytes 12292
  162.7 23.9 %copy-start = (bf16[2,512,16,64]{1,3,2,0:T(8,128)(2,1)}, bf16[2,512,16,64]{1,3,2,0:T(8,128)(2,1)S(1)}, u32[]{:S(2)}) copy-start(bf16[2,512,16,64]{1,3,2,0:T(8,128)(2,1)S(1)} %copy.57) | copy-start | bytes 6291460
  201.6 13.9 %copy-start.5 = (bf16[2,512,16,64]{1,3,2,0:T(8,128)(2,1)S(1)}, bf16[2,512,16,64]{1,3,2,0:T(8,128)(2,1)}, u32[]{:S(2)}) copy-start(bf16[2,512,16,64]{1,3,2,0:T(8,128)(2,1)} %copy.58) | copy-start | bytes 6291460
  229.5 2.8 copy-start.3
  229.5 2.8 copy-start.21
  231.7 3.5 slice-start
  232.3 2.9 copy-start.13
  232.3 3.5 slice-start.1
  235.8 49.8 %copy-start.11 = (bf16[2,512,1024]{2,1,0:T(8,128)(2,1)S(1)}, bf16[2,512,1024]{2,1,0:T(8,128)(2,1)}, u32[]{:S(2)}) copy-start(bf16[2,512,1024]{2,1,0:T(8,128)(2,1)} %param.13) | copy-start | bytes 6291460
  285.7 24.0 %copy-start.20 = (f32[1024]{0:T(1024)S(1)}, f32[1024]{0:T(1024)}, u32[]{:S(2)}) copy-start(f32[1024]{0:T(1024)} %reshape.371) | copy-start | bytes 12292
  355.2 20.1 %copy-start.7 = (f32[1024,1024]{1,0:T(8,128)}, f32[1024,1024]{1,0:T(8,128)S(1)}, u32[]{:S(2)}) copy-start(f32[1024,1024]{1,0:T(8,128)S(1)} %multiply_add_fusion) | copy-start | bytes 12582916
  355.2 16.4 %copy-start.14 = (bf16[128,8,2,512]{3,1,2,0:T(8,128)(2,1)S(1)}, bf16[128,8,2,512]{3,1,2,0:T(8,128)(2,1)}, u32[]{:S(2)}) copy-start(bf16[128,8,2,512]{3,1,2,0:T(8,128)(2,1)} %copy-done.13) | copy-start | bytes 6291460
  371.6 3.6 copy-start.22
  377.8 8.4 %copy-start.12 = (f32[2,16,512]{2,1,0:T(8,128)S(1)}, f32[2,16,512]{2,1,0:T(8,128)}, u32[]{:S(2)}) copy-start(f32[2,16,512]{2,1,0:T(8,128)} %log_add_fusion) | copy-start | bytes 196612
  401.6 5.8 copy-start.6
  457.5 13.0 %copy-start.1 = (bf16[2,512,16,64]{1,3,2,0:T(8,128)(2,1)S(1)}, bf16[2,512,16,64]{1,3,2,0:T(8,128)(2,1)}, u32[]{:S(2)}) copy-start(bf16[2,512,16,64]{1,3,2,0:T(8,128)(2,1)} %copy-done) | copy-start | bytes 6291460
  479.1 2.8 copy-start.9
  481.9 4.0 slice-start.2
  484.1 1.6 copy-start.10
  484.7 1.6 copy-start.4
  484.7 1.6 copy-start.17
  484.7 1.6 copy-start.19
  484.7 2.2 slice-start.3
  495.1 8.7 %copy-start.8 = (f32[1024,1024]{1,0:T(8,128)S(1)}, f32[1024,1024]{1,0:T(8,128)}, u32[]{:S(2)}) copy-start(f32[1024,1024]{1,0:T(8,128)} %copy-done.7) | copy-start | bytes 12582916
  503.8 2.7 copy-start.15
  503.8 2.7 copy-start.18

commit v2 on v1

--- a/solution.py
+++ b/solution.py
@@ -229,180 +229,237 @@
     )(*parts)
 
 
-D = 1024
-HEADS = 16
-HEAD_DIM = 64
-
-
 EPS = 1e-06
-
-
-def build_mask(span, length):
-    slots = jnp.arange(span.shape[0], dtype=jnp.int32)
-    ends = jnp.sum(jnp.where(slots[:, None] <= slots[None, :], span[:, None], 0), axis=0)
-    position = jnp.arange(length, dtype=jnp.int32)
-    segment = jnp.sum((position[:, None] >= ends[None, :]).astype(jnp.int32), axis=1)
-    same = segment[:, None] == segment[None, :]
-    return jnp.logical_and(same, position[:, None] >= position[None, :])
-
-
-def normalize(x_val):
-    factor = lax.rsqrt(jnp.mean(x_val * x_val, axis=-1, keepdims=True) + EPS)
-    return (x_val * factor, factor)
-
-
-def norm_back(normal, factor, gain, grad_out):
-    gain_grad = jnp.sum(grad_out * normal, axis=0)
-    scaled = grad_out * gain
-    inner = jnp.mean(scaled * normal, axis=-1, keepdims=True)
-    return (factor * (scaled - normal * inner), gain_grad)
-
-
-def split_heads(project, count):
-    queries = project[:, :D].reshape(count, -1, HEADS, HEAD_DIM)
-    key_rows = project[:, D : 2 * D].reshape(count, -1, HEADS, HEAD_DIM)
-    value_rows = project[:, 2 * D :].reshape(count, -1, HEADS, HEAD_DIM)
-    return (queries, key_rows, value_rows)
-
-
-def masked_scores(queries, key_rows, mask):
-    scores = (
-        jnp.einsum("bqhd,bkhd->bhqk", queries, key_rows, preferred_element_type=jnp.float32) * 0.125
-    )
-    return jnp.where(mask[:, None], scores, -1e30)
-
-
-def exact_gelu(value):
-    return jax.nn.gelu(value, approximate=False)
-
-
-def forward_pass(x_val, mask, params):
-    first_gain, qkv_weight, out_weight, second_gain, up_weight, up_bias, down_weight, down_bias = (
-        params
-    )
-    count = x_val.shape[0]
-    normal_in, factor_in = normalize(x_val)
-    entered = (normal_in * first_gain.astype(jnp.float32)).astype(jnp.bfloat16)
-    project = jnp.dot(entered, qkv_weight, preferred_element_type=jnp.float32).astype(jnp.bfloat16)
-    queries, key_rows, value_rows = split_heads(project, mask.shape[0])
-    scores = masked_scores(queries, key_rows, mask)
-    peak = jnp.max(scores, axis=-1, keepdims=True)
-    expo = jnp.exp(scores - peak)
-    total = jnp.sum(expo, axis=-1, keepdims=True)
-    logsum = peak + jnp.log(total)
-    attend = (expo / total).astype(jnp.bfloat16)
-    attended = jnp.einsum("bhqk,bkhd->bqhd", attend, value_rows, preferred_element_type=jnp.float32)
-    attended = attended.reshape(count, D).astype(jnp.bfloat16)
-    middle = x_val + jnp.dot(attended, out_weight, preferred_element_type=jnp.float32)
-    normal_mid, factor_mid = normalize(middle)
-    second = (normal_mid * second_gain.astype(jnp.float32)).astype(jnp.bfloat16)
-    hidden = jnp.dot(second, up_weight, preferred_element_type=jnp.float32) + up_bias.astype(
-        jnp.float32
-    )
-    active = exact_gelu(hidden).astype(jnp.bfloat16)
-    final = jnp.dot(active, down_weight, preferred_element_type=jnp.float32) + down_bias.astype(
-        jnp.float32
-    )
-    kept = (
-        normal_in,
-        factor_in,
-        entered,
-        project,
-        logsum,
-        attended,
-        normal_mid,
-        factor_mid,
-        second,
-        hidden,
-        active,
-    )
-    return (middle + final, kept)
-
-
-def backward_pass(grad, mask, params, kept):
-    first_gain, qkv_weight, out_weight, second_gain, up_weight, up_bias, down_weight, down_bias = (
-        params
-    )
-    (
-        normal_in,
-        factor_in,
-        entered,
-        project,
-        logsum,
-        attended,
-        normal_mid,
-        factor_mid,
-        second,
-        hidden,
-        active,
-    ) = kept
-    count = grad.shape[0]
-    grad_final = grad.astype(jnp.bfloat16)
-    down_bias_grad = jnp.sum(grad_final.astype(jnp.float32), axis=0)
-    down_grad = jnp.einsum("rf,rd->fd", active, grad_final, preferred_element_type=jnp.float32)
-    grad_active = jnp.einsum(
-        "rd,fd->rf", grad_final, down_weight, preferred_element_type=jnp.float32
-    )
-    gelu_value, gelu_back = jax.vjp(exact_gelu, hidden)
-    grad_hidden = gelu_back(grad_active)[0].astype(jnp.bfloat16)
-    up_bias_grad = jnp.sum(grad_hidden.astype(jnp.float32), axis=0)
-    up_grad = jnp.einsum("rd,rf->df", second, grad_hidden, preferred_element_type=jnp.float32)
-    grad_second = jnp.einsum(
-        "rf,df->rd", grad_hidden, up_weight, preferred_element_type=jnp.float32
-    )
-    grad_norm_mid, second_gain_grad = norm_back(
-        normal_mid, factor_mid, second_gain.astype(jnp.float32), grad_second
-    )
-    grad_middle = grad + grad_norm_mid
-    grad_branch = grad_middle.astype(jnp.bfloat16)
-    out_grad = jnp.einsum("re,rd->ed", attended, grad_branch, preferred_element_type=jnp.float32)
-    grad_attended = jnp.einsum(
-        "rd,ed->re", grad_branch, out_weight, preferred_element_type=jnp.float32
-    )
-    grad_attended = grad_attended.astype(jnp.bfloat16).reshape(mask.shape[0], -1, HEADS, HEAD_DIM)
-    queries, key_rows, value_rows = split_heads(project, mask.shape[0])
-    scores = masked_scores(queries, key_rows, mask)
-    attend_full = jnp.exp(scores - logsum)
-    attend = attend_full.astype(jnp.bfloat16)
-    value_grad = jnp.einsum(
-        "bhqk,bqhd->bkhd", attend, grad_attended, preferred_element_type=jnp.float32
-    )
-    grad_attend = jnp.einsum(
-        "bqhd,bkhd->bhqk", grad_attended, value_rows, preferred_element_type=jnp.float32
-    )
-    row_total = jnp.sum(attend_full * grad_attend, axis=-1, keepdims=True)
-    grad_scores = (attend_full * (grad_attend - row_total)).astype(jnp.bfloat16)
-    query_grad = (
-        jnp.einsum("bhqk,bkhd->bqhd", grad_scores, key_rows, preferred_element_type=jnp.float32)
-        * 0.125
-    )
-    key_grad = (
-        jnp.einsum("bhqk,bqhd->bkhd", grad_scores, queries, preferred_element_type=jnp.float32) * 0.125
-    )
-    grad_project = jnp.concatenate(
-        (query_grad.reshape(count, D), key_grad.reshape(count, D), value_grad.reshape(count, D)),
-        axis=1,
-    )
-    grad_project = grad_project.astype(jnp.bfloat16)
-    qkv_grad = jnp.einsum("rd,re->de", entered, grad_project, preferred_element_type=jnp.float32)
-    grad_entered = jnp.einsum(
-        "re,de->rd", grad_project, qkv_weight, preferred_element_type=jnp.float32
-    )
-    grad_norm_in, first_gain_grad = norm_back(
-        normal_in, factor_in, first_gain.astype(jnp.float32), grad_entered
-    )
-    frames_grad = grad_middle + grad_norm_in
-    grads = (
-        first_gain_grad,
-        qkv_grad,
-        out_grad,
-        second_gain_grad,
-        up_grad,
-        up_bias_grad,
-        down_grad,
-        down_bias_grad,
-    )
-    return (frames_grad, grads)
+BLOCK = 1024
+TALL = 256
+NT = (((1,), (1,)), ((), ()))
+TN = (((0,), (0,)), ((), ()))
+NN = (((1,), (0,)), ((), ()))
+F32, BF16 = jnp.float32, jnp.bfloat16
+
+
+def mul(a, b, dims=NN):
+    return lax.dot_general(a, b, dims, preferred_element_type=F32)
+
+
+def mlp_kernel(middle, cot, gain, up, up_b, down, down_b, out, grad_middle, grad_branch, up_g, down_g, up_b_g, gain_g, down_b_g,
+               second, total, back, active, grad_hidden):
+    step, last = pl.program_id(0), pl.num_programs(0) - 1
+    rows, width = middle.shape
+    part = 128
+
+    @pl.when(step == 0)
+    def _():
+        @pl.loop(0, rows // part)
+        def _(i):
+            at = pl.ds(pl.multiple_of(i * part, part), part)
+            x = middle[at, :]
+            normal = x * lax.rsqrt(jnp.mean(x * x, axis=-1, keepdims=True) + EPS)
+            second[at, :] = (normal * gain[...]).astype(BF16)
+
+    bias = up_b[...]
+    up_b_g[...] = jnp.zeros_like(up_b_g)
+
+    @pl.loop(0, rows // TALL)
+    def _(i):
+        at = pl.ds(pl.multiple_of(i * TALL, TALL), TALL)
+        hidden = mul(second[at, :], up[...]) + bias
+        grad = mul(cot[at, :], down[...], NT)
+        half = 0.5 + 0.5 * lax.erf(hidden * (0.5 ** 0.5))
+        slope = half + hidden * (jnp.exp(hidden * hidden * -0.5) * 0.3989422804014327)
+        active[at, :] = (hidden * half).astype(BF16)
+        low = (grad * slope).astype(BF16)
+        grad_hidden[at, :] = low
+        up_b_g[...] += jnp.sum(low.astype(F32), axis=0, keepdims=True)
+
+    @pl.loop(0, rows // TALL)
+    def _(i):
+        at = pl.ds(pl.multiple_of(i * TALL, TALL), TALL)
+        more, less = mul(active[at, :], down[...]), mul(grad_hidden[at, :], up[...], NT)
+
+        @pl.when(step == 0)
+        def _():
+            total[at, :] = more
+            back[at, :] = less
+
+        @pl.when(step > 0)
+        def _():
+            total[at, :] += more
+            back[at, :] += less
+
+    @pl.loop(0, BLOCK // TALL)
+    def _(i):
+        at = pl.ds(pl.multiple_of(i * TALL, TALL), TALL)
+        down_g[at, :] = mul(active[:, at], cot[...], TN).astype(down_g.dtype)
+
+    @pl.loop(0, width // TALL)
+    def _(i):
+        at = pl.ds(pl.multiple_of(i * TALL, TALL), TALL)
+        up_g[at, :] = mul(second[:, at], grad_hidden[...], TN).astype(up_g.dtype)
+
+    @pl.when(step == last)
+    def _():
+        gain_g[...] = jnp.zeros_like(gain_g)
+        down_b_g[...] = jnp.zeros_like(down_b_g)
+
+        @pl.loop(0, rows // part)
+        def _(i):
+            at = pl.ds(pl.multiple_of(i * part, part), part)
+            x = middle[at, :]
+            factor = lax.rsqrt(jnp.mean(x * x, axis=-1, keepdims=True) + EPS)
+            normal = x * factor
+            out[at, :] = (x + (total[at, :] + down_b[...])).astype(BF16)
+            g = cot[at, :].astype(F32)
+            grad = back[at, :]
+            gain_g[...] += jnp.sum(grad * normal, axis=0, keepdims=True)
+            down_b_g[...] += jnp.sum(g, axis=0, keepdims=True)
+            n = grad * gain[...]
+            result = g + factor * (n - normal * jnp.mean(n * normal, axis=-1, keepdims=True))
+            grad_middle[at, :] = result
+            grad_branch[at, :] = result.astype(BF16)
+
+
+def mlp(middle, cot, gain, up, up_b, down, down_b, sum_type=BF16):
+    rows, width = middle.shape
+    ff = up.shape[1]
+    whole = lambda *s: pl.BlockSpec(s, lambda j: (0,) * len(s), pipeline_mode=pl.Buffered(1))
+    row = whole(1, width)
+    return pl.pallas_call(
+        mlp_kernel,
+        grid=(ff // BLOCK,),
+        in_specs=[whole(rows, width), whole(rows, width), row, pl.BlockSpec((width, BLOCK), lambda j: (0, j)),
+                  pl.BlockSpec((1, BLOCK), lambda j: (0, j)), pl.BlockSpec((BLOCK, width), lambda j: (j, 0)), row],
+        out_specs=[whole(rows, width), whole(rows, width), whole(rows, width), pl.BlockSpec((width, BLOCK), lambda j: (0, j)),
+                   pl.BlockSpec((BLOCK, width), lambda j: (j, 0)), pl.BlockSpec((1, BLOCK), lambda j: (0, j)), row, row],
+        out_shape=[jax.ShapeDtypeStruct(s, d) for s, d in (
+            ((rows, width), BF16), ((rows, width), F32), ((rows, width), BF16), ((width, ff), sum_type), ((ff, width), sum_type),
+            ((1, ff), F32), ((1, width), F32), ((1, width), F32))],
+        scratch_shapes=[pltpu.VMEM((rows, width), BF16), pltpu.VMEM((rows, width), F32), pltpu.VMEM((rows, width), F32),
+                        pltpu.VMEM((rows, BLOCK), BF16), pltpu.VMEM((rows, BLOCK), BF16)],
+        compiler_params=pltpu.CompilerParams(vmem_limit_bytes=56 * 2 ** 20, dimension_semantics=("arbitrary",)),
+        name="mlp",
+    )(middle, cot, gain.reshape(1, -1).astype(F32), up, up_b.reshape(1, -1).astype(F32), down, down_b.reshape(1, -1).astype(F32))
+
+
+PIECE = 128
+REACH = 256
+
+
+def spans(rows):
+    return [(max(0, i * PIECE - REACH), i * PIECE, (i + 1) * PIECE) for i in range(rows // PIECE)]
+
+
+def side_by_side(x, lanes):
+    zero = jnp.zeros_like(x)
+    return jnp.concatenate([jnp.where(lanes, x, zero), jnp.where(lanes, zero, x)], axis=0)
+
+
+def fill_bias(bias, start, rows):
+    at = 0
+    for low, q, high in spans(rows):
+        n = high - low
+        key = low + lax.broadcasted_iota(jnp.int32, (n, PIECE), 0)
+        query = q + lax.broadcasted_iota(jnp.int32, (n, PIECE), 1)
+        seen = jnp.logical_and(key <= query, key >= start[:, q:high])
+        b = jnp.where(seen, 0.0, -1e30)
+        bias[at:at + n, :] = jnp.concatenate([b, b], axis=1)
+        at += n
+
+
+def attend_kernel(q_ref, k_ref, v_ref, start, out, logsum, bias):
+    rows, wide = q_ref.shape
+
+    @pl.when(pl.program_id(1) == 0)
+    def _():
+        fill_bias(bias, start[0], rows)
+
+    lanes = lax.broadcasted_iota(jnp.int32, (PIECE, wide), 1) < wide // 2
+    at = 0
+    for i, (low, q, high) in enumerate(spans(rows)):
+        n = high - low
+        queries = side_by_side(q_ref[q:high, :] * 0.125, lanes)
+        scores = mul(k_ref[low:high, :], queries, NT) + bias[at:at + n, :]
+        peak = jnp.max(scores, axis=0, keepdims=True)
+        expo = jnp.exp(scores - peak)
+        total = jnp.sum(expo, axis=0, keepdims=True)
+        logsum[0, 0, i:i + 1, :] = peak + jnp.log(total)
+        attend = (expo * (1.0 / total)).astype(BF16)
+        both = mul(attend, v_ref[low:high, :], TN)
+        out[q:high, :] = jnp.where(lanes, both[:PIECE], both[PIECE:]).astype(BF16)
+        at += n
+
+
+def attend_specs(rows, pairs):
+    block = lambda off: pl.BlockSpec((rows, 128), lambda b, h: (b, off * pairs + h))
+    start = pl.BlockSpec((1, 1, rows), lambda b, h: (b, 0, 0))
+    logsum = pl.BlockSpec((1, 1, rows // PIECE, 2 * PIECE), lambda b, h: (b, h, 0, 0))
+    return block, start, logsum
+
+
+def attend(project, start):
+    batches, rows = start.shape[0], start.shape[2]
+    width = project.shape[1] // 3
+    pairs = width // 128
+    block, start_spec, logsum = attend_specs(rows, pairs)
+    return pl.pallas_call(
+        attend_kernel,
+        grid=(batches, pairs),
+        in_specs=[block(0), block(1), block(2), start_spec],
+        out_specs=[block(0), logsum],
+        out_shape=[jax.ShapeDtypeStruct((batches * rows, width), BF16),
+                   jax.ShapeDtypeStruct((batches, pairs, rows // PIECE, 2 * PIECE), F32)],
+        scratch_shapes=[pltpu.VMEM((sum(h - l for l, _, h in spans(rows)), 2 * PIECE), F32)],
+        compiler_params=pltpu.CompilerParams(vmem_limit_bytes=40 * 2 ** 20, dimension_semantics=("arbitrary", "arbitrary")),
+        name="attend",
+    )(project, project, project, start)
+
+
+def attend_back_kernel(q_ref, k_ref, v_ref, g_ref, start, logsum, out, bias, k_sum, v_sum):
+    rows, wide = q_ref.shape
+
+    @pl.when(pl.program_id(1) == 0)
+    def _():
+        fill_bias(bias, start[0], rows)
+
+    lanes = lax.broadcasted_iota(jnp.int32, (PIECE, wide), 1) < wide // 2
+    at = 0
+    k_sum[...] = jnp.zeros_like(k_sum)
+    v_sum[...] = jnp.zeros_like(v_sum)
+    for i, (low, q, high) in enumerate(spans(rows)):
+        n = high - low
+        queries = side_by_side(q_ref[q:high, :] * 0.125, lanes)
+        grads = side_by_side(g_ref[q:high, :], lanes)
+        keys, values = k_ref[low:high, :], v_ref[low:high, :]
+        scores = mul(keys, queries, NT) + bias[at:at + n, :]
+        full = jnp.exp(scores - logsum[0, 0, i:i + 1, :])
+        grad = mul(values, grads, NT)
+        v_sum[low:high, :] += mul(full.astype(BF16), grads)
+        total = jnp.sum(full * grad, axis=0, keepdims=True)
+        grad_scores = (full * (grad - total)).astype(BF16)
+        k_sum[low:high, :] += mul(grad_scores, queries)
+        both = mul(grad_scores, keys, TN) * 0.125
+        out[0, q:high, :] = jnp.where(lanes, both[:PIECE], both[PIECE:]).astype(BF16)
+        at += n
+    out[1] = k_sum[...].astype(BF16)
+    out[2] = v_sum[...].astype(BF16)
+
+
+def attend_back(project, grad, start, logsum):
+    batches, rows = start.shape[0], start.shape[2]
+    width = project.shape[1] // 3
+    pairs = width // 128
+    block, start_spec, logsum_spec = attend_specs(rows, pairs)
+    return pl.pallas_call(
+        attend_back_kernel,
+        grid=(batches, pairs),
+        in_specs=[block(0), block(1), block(2), block(0), start_spec, logsum_spec],
+        out_specs=pl.BlockSpec((3, rows, 128), lambda b, h: (0, b, h)),
+        out_shape=jax.ShapeDtypeStruct((3, batches * rows, width), BF16),
+        scratch_shapes=[pltpu.VMEM((sum(h - l for l, _, h in spans(rows)), 2 * PIECE), F32),
+                        pltpu.VMEM((rows, 128), F32), pltpu.VMEM((rows, 128), F32)],
+        compiler_params=pltpu.CompilerParams(vmem_limit_bytes=40 * 2 ** 20, dimension_semantics=("arbitrary", "arbitrary")),
+        name="attend_back",
+    )(project, project, project, grad, start, logsum)
 
 
 def pack(vectors, owners, rows):
@@ -421,6 +478,50 @@
 
 def fits(sizes, shards):
     return all(s & (s - 1) == 0 for s in sizes.values()) and all(a.shape[0] % 16 == 0 for a in shards)
+
+
+def item_ends(lengths):
+    slots = jnp.arange(lengths.shape[1], dtype=jnp.int32)
+    ends = jnp.sum(jnp.where(slots[None, :, None] <= slots[None, None, :], lengths[:, :, None], 0), axis=1)
+    return ends
+
+
+def normalize(x_val):
+    factor = lax.rsqrt(jnp.mean(x_val * x_val, axis=-1, keepdims=True) + EPS)
+    return (x_val * factor, factor)
+
+
+def norm_back(normal, factor, gain, grad_out):
+    gain_grad = jnp.sum(grad_out * normal, axis=0)
+    scaled = grad_out * gain
+    inner = jnp.mean(scaled * normal, axis=-1, keepdims=True)
+    return (factor * (scaled - normal * inner), gain_grad)
+
+
+def block_pass(frames, lengths, cotangent, params, sum_type):
+    first, qkv, out, second, up, up_b, down, down_b = params
+    batches, rows, width = frames.shape
+    x_val = frames.reshape(batches * rows, width).astype(F32)
+    cot = cotangent.reshape(batches * rows, width)
+    ends = item_ends(lengths)
+    position = jnp.arange(rows, dtype=jnp.int32)[None, None, :]
+    start = jnp.max(jnp.where(ends[:, :, None] <= position, ends[:, :, None], 0), axis=1, keepdims=True)
+    normal, factor = normalize(x_val)
+    gain = first.astype(F32)
+    entered = (normal * gain).astype(BF16)
+    project = mul(entered, qkv).astype(BF16)
+    attended, logsum = attend(project, start)
+    middle = x_val + mul(attended, out)
+    output, grad_middle, grad_branch, up_g, down_g, up_b_g, second_g, down_b_g = mlp(middle, cot, second, up, up_b, down, down_b, sum_type)
+    out_g = mul(attended, grad_branch, TN)
+    grad_attended = mul(grad_branch, out, NT).astype(BF16)
+    grads = attend_back(project, grad_attended, start, logsum)
+    qkv_g = [mul(entered, grads[j], TN) for j in range(3)]
+    grad_entered = sum(mul(grads[j], qkv[:, j * width:(j + 1) * width], NT) for j in range(3))
+    back, first_g = norm_back(normal, factor, gain, grad_entered)
+    shape = frames.shape
+    return (output.reshape(shape), (grad_middle + back).reshape(shape), (down_g, up_g, out_g, *qkv_g),
+            (first_g, second_g.reshape(-1), up_b_g.reshape(-1), down_b_g.reshape(-1)))
 
 
 def body(sizes, frames, lengths, cotangent, *shards):
@@ -436,21 +537,14 @@
         qkv, out, up, down = [lax.all_gather(w, AXES, axis=0, tiled=True) for w in weights]
         first, second, up_b, down_b = [lax.all_gather(v, AXES, axis=0, tiled=True) for v in vectors]
     params = (first, qkv, out, second, up, up_b, down, down_b)
-    batches, rows, width = frames.shape
-    mask = jnp.stack([build_mask(lengths[b, 0], rows) for b in range(batches)])
-    output, kept = forward_pass(frames.reshape(batches * rows, width).astype(jnp.float32), mask, params)
-    frames_grad, grads = backward_pass(cotangent.reshape(batches * rows, width).astype(jnp.float32), mask, params, kept)
-    big = [grads[i] for i in (1, 2, 4, 6)]
-    small = [grads[i] for i in (0, 3, 5, 7)]
+    output, frames_grad, big, small = block_pass(frames, lengths[:, 0], cotangent, params, BF16 if own_kernels else F32)
     if own_kernels:
-        big = [g.astype(jnp.bfloat16) for g in (big[3], big[2], big[1], big[0])]
-        down_g, up_g, out_g, qkv_g, packed = scatter(big + [pack(small, owners, 8)], sizes, 2)
+        down_g, up_g, out_g, *qkv_g, packed = scatter([g.astype(BF16) for g in big] + [pack(small, owners, 8)], sizes, 2)
         first_g, second_g, up_b_g, down_b_g = unpack(packed, 1, widths)
     else:
-        qkv_g, out_g, up_g, down_g = [lax.psum_scatter(g.astype(jnp.float32), AXES, scatter_dimension=0, tiled=True) for g in big]
+        down_g, up_g, out_g, *qkv_g = [lax.psum_scatter(g.astype(F32), AXES, scatter_dimension=0, tiled=True) for g in big]
         first_g, second_g, up_b_g, down_b_g = [lax.psum_scatter(g, AXES, scatter_dimension=0, tiled=True) for g in small]
-    shape = (batches, rows, width)
-    return (output.astype(jnp.bfloat16).reshape(shape), frames_grad.reshape(shape), first_g, qkv_g, out_g, second_g, up_g, up_b_g, down_g, down_b_g)
+    return (output, frames_grad, first_g, jnp.concatenate(qkv_g, axis=1), out_g, second_g, up_g, up_b_g, down_g, down_b_g)
 
 
 def solution(mesh):

time: 649 us -> 459 us (0.71)
  matrix products: 258 us -> 46.4 us
  Pallas kernels: 257 us -> 390 us
  local copies, waits for them, and re-layouts: 74.6 us -> 8.66 us
  other arithmetic: 53.2 us -> 12.7 us
    dot_general x18 -> x10, matrix products: 258 us -> 46.4 us  [mul(): return lax.dot_general(a, b, dims, preferred_element_type=F32)]
    pallas_call x0 -> x3, Pallas kernels: none -> 132 us  [the longest x1 83.2 us: mlp(): pl.pallas_call(mlp_kernel, grid=(ff // BLOCK,), in_specs=[whole(rows, wid...]
    reshape x8 -> x0, local copies, waits for them, and re-layouts: 40.7 us -> none  [the longest x2 12.1 us: split_heads(): queries = project[:, :D].reshape(count, -1, HEADS, HEAD_DIM)]
    convert_element_type x4 -> x3, other arithmetic: 28.6 us -> 1.3 us  [the longest x1 0.68 us: mlp(): up_b.reshape(1, -1).astype(F32)]
    reduce_sum x5 -> x1, other arithmetic: 15.5 us -> 0.09 us  [item_ends(): jnp.sum(jnp.where(slots[None, :, None] <= slots[None, None, :], lengths[:...]
    unnamed x67 -> x52, local copies, waits for them, and re-layouts: 15.7 us -> 3.97 us
where the time goes in v2:
time: 459 us; the launch traced here: 458 us
  Pallas kernels  390 us (85%)
  matrix products  46.4 us (10%)
  other arithmetic  12.7 us (3%)
  local copies, waits for them, and re-layouts  8.66 us (2%)
    pallas_call x1, Pallas kernels, gather(): pl.pallas_call(functools.partial(gather_kernel, table, len(shards), chunk...  130 us
    pallas_call x1, Pallas kernels, scatter(): pl.pallas_call(functools.partial(scatter_kernel, table, plan), out_shape=...  127 us
    pallas_call x1, Pallas kernels, mlp(): pl.pallas_call(mlp_kernel, grid=(ff // BLOCK,), in_specs=[whole(rows, wid...  83.2 us
    dot_general x10, matrix products, mul(): return lax.dot_general(a, b, dims, preferred_element_type=F32)  46.4 us
    pallas_call x1, Pallas kernels, attend_back(): pl.pallas_call(attend_back_kernel, grid=(batches, pairs), in_specs=[block...  28.9 us
    pallas_call x1, Pallas kernels, attend(): pl.pallas_call(attend_kernel, grid=(batches, pairs), in_specs=[block(0),...  20.3 us

profile of v2, /device:TPU:0, one launch (start us, length us, event | category | flops | bytes accessed | tf_op | source)
XLA Modules:
  0.0 458.2 jit_solution(628000525362268268)
XLA Ops:
  0.6 0.0 copy-start.2
  0.7 1.5 fusion.20
  2.2 130.2 %gather.1 = (bf16[2,2,2,2,2,16,128]{6,5,4,3,2,1,0:T(8,128)(2,1)}, bf16[2,2,2,2,2,32,3072]{6,5,4,3,2,1,0:T(8,128)(2,1)}, bf16[2,2,2,2,2,32,1024]{6,5,4,3,2,1,0:T(...) custom-call(bf16[16,128]{1,0:T(8,128)(2,1)} %bitcast.110, ...), custom_call_target="tpu_custom_call" | custom-call | tf_op jit(solution)/shard_map/gather/pallas_call | solution.py:113
  132.4 0.9 copy.25
  133.4 0.1 slice_convert_fusion
  133.4 0.1 reshape.252
  133.5 2.1 fusion.8
  135.6 0.5 fusion.10
  136.2 0.0 copy-start.15
  136.2 10.4 %convolution_convert_fusion.q_ref.k_ref.v_ref = bf16[1024,3072]{1,0:T(8,128)(2,1)S(1)} fusion(bf16[1024,1024]{1,0:T(8,128)(2,1)S(1)} %bitcast.101, bf16[1024,3072]{1,0:T(8,128)(2,1)} %bitcast.121), kind=kOutput, calls=%fused_computation | convolution fusion | flops 6445596672 | bytes 14680064 | tf_op jit(solution)/shard_map/dot_general | solution.py:242
  146.6 0.1 select_reduce_fusion.1
  146.7 0.1 select_reduce_fusion
  146.8 0.0 copy-start.3
  146.9 20.3 %attend.1 = (bf16[1024,1024]{1,0:T(8,128)(2,1)S(1)}, f32[2,8,4,256]{3,2,1,0:T(4,128)S(1)}) custom-call(bf16[1024,3072]{1,0:T(8,128)(2,1)S(1)} %convolution_convert_fusion.q_ref.k_ref.v_ref, bf16[1024,3072]{1,0:T(8,128)(2,1)S(1)} %convolution_convert_fusion.q_ref.k_ref.v_ref, bf16[1024,3072]{1,0:T(8,128)(2,1)S(1)} %convolution_convert_fusion.q_ref.k_ref.v_ref, ...), custom_call_target="tpu_custom_call" | custom-call | tf_op jit(solution)/shard_map/attend/pallas_call | solution.py:404
  167.2 4.4 bitcast_add_fusion.middle
  171.6 0.7 reshape.253.gain
  172.3 0.7 reshape.255.down_b
  173.0 0.7 slice_convert_fusion.1
  173.7 83.2 %mlp.1 = (bf16[1024,1024]{1,0:T(8,128)(2,1)}, f32[1024,1024]{1,0:T(8,128)}, bf16[1024,1024]{1,0:T(8,128)(2,1)}, bf16[1024,4096]{1,0:T(8,128)(2,1)}, bf16[4096,10...) custom-call(f32[1024,1024]{1,0:T(8,128)} %bitcast_add_fusion.middle, ...), custom_call_target="tpu_custom_call" | custom-call | tf_op jit(solution)/shard_map/mlp/pallas_call | solution.py:327
  256.9 0.0 slice-start.2
  256.9 4.1 convolution_convert_fusion.5.g_ref
  261.0 0.0 slice-start.3
  261.0 28.9 %attend_back.1 = bf16[3,1024,1024]{2,1,0:T(8,128)(2,1)S(1)} custom-call(bf16[1024,3072]{1,0:T(8,128)(2,1)} %copy-done, bf16[1024,3072]{1,0:T(8,128)(2,1)} %copy-done, bf16[1024,3072]{1,0:T(8,128)(2,1)} %copy-done, bf16[1024,1024]{1,0:T(8,128)(2,1)S(1)} %convolution_convert_fusion.5.g_ref, s32[2,1,512]{2,1,0:T(1,128)S(1)} %broadcast_in_dim.49.start, ...), custom_call_target="tpu_custom_call" | custom-call | tf_op jit(solution)/shard_map/attend_back/pallas_call | solution.py:452
  289.9 2.4 fusion.13
  292.3 0.0 copy-start.4
  292.3 2.4 fusion.11
  294.7 0.0 copy-start.12
  294.8 5.1 %fusion.7 = (f32[1024]{0:T(1024)S(1)}, f32[1024]{0:T(1024)S(1)}, f32[1024,1024]{1,0:T(8,128)}) fusion(bf16[2,512,1024]{2,1,0:T(8,128)(2,1)S(1)} %copy-done.4, f32[1024]{0:T(1024)S(1)} %bitcast.112, f32[1024]{0:T(1024)S(1)} %reshape.252, f32[1024,1024]{1,0:T(8,128)S(1)} %fusion.11, f32[1024,1024]{1,0:T(8,128)S(1)} %fusion.13, ...), kind=kOutput, calls=%fused_computation.12 | convolution fusion | flops 2156918784 | bytes 18890752 | tf_op jit(solution)/shard_map/dot_general | solution.py:242
  299.8 0.1 reshape.245
  299.9 0.5 broadcast.99
  300.4 0.7 reduce.10
  301.1 0.1 reshape_reshape.19
  301.1 0.7 reduce.9
  301.8 0.1 reshape_reshape.21
  301.9 0.1 fusion.19
  302.0 0.7 copy.23
  302.7 6.3 %convolution_convert_fusion.1 = bf16[1024,1024]{1,0:T(8,128)(2,1)} fusion(bf16[1024,1024]{1,0:T(8,128)(2,1)} %bitcast.102, bf16[3,1024,1024]{2,1,0:T(8,128)(2,1)} %copy-done.1), kind=kOutput, calls=%fused_computation.26 | convolution fusion | flops 2148532224 | bytes 6291456 | tf_op jit(solution)/shard_map/dot_general | solution.py:242
  309.0 3.8 convolution_convert_fusion.2
  312.8 3.8 convolution_convert_fusion.3
  316.6 3.8 convolution_convert_fusion.4
  320.3 126.9 %scatter.1 = (f32[128,1024]{1,0:T(8,128)}, f32[32,4096]{1,0:T(8,128)}, f32[32,1024]{1,0:T(8,128)}, f32[32,1024]{1,0:T(8,128)}, f32[32,1024]{1,0:T(8,128)}, /*index=5*/f32[32,1024]{1,0:T(8,128)}, f32[8,128]{1,0:T(8,128)}) custom-call(bf16[2,2,2,2,2,128,1024]{6,5,4,3,2,1,0:T(8,128)(2,1)} %bitcast.92, bf16[2,2,2,2,2,32,4096]{6,5,4,3,2,1,0:T(8,128)(2,1)} %bitcast.91, ...), custom_call_target="tpu_custom_call" | custom-call | tf_op jit(solution)/shard_map/scatter/pallas_call | solution.py:221
  447.2 1.8 pad_maximum_fusion
  449.1 1.3 slice_bitcast_fusion.11
  450.3 1.3 slice_bitcast_fusion.12
  451.6 4.4 fusion.6
  456.0 0.7 copy.29
  456.7 0.8 copy.30
  457.5 0.8 copy.31
  (46 shorter events, 0.1 us)
Async XLA Ops:
  0.6 135.0 %copy-start.2 = (bf16[2,512,1024]{2,1,0:T(8,128)(2,1)S(1)}, bf16[2,512,1024]{2,1,0:T(8,128)(2,1)}, u32[]{:S(2)}) copy-start(bf16[2,512,1024]{2,1,0:T(8,128)(2,1)} %param.11) | copy-start | bytes 6291460
  136.2 10.4 %copy-start.7 = (bf16[2,512,1024]{2,1,0:T(8,128)(2,1)}, bf16[2,512,1024]{2,1,0:T(8,128)(2,1)S(1)}, u32[]{:S(2)}) copy-start(bf16[2,512,1024]{2,1,0:T(8,128)(2,1)S(1)} %fusion.10) | copy-start | bytes 6291460
  136.2 10.5 %copy-start.15 = (s32[2,1,16]{2,1,0:T(1,128)S(1)}, s32[2,1,16]{2,1,0:T(1,128)}, u32[]{:S(2)}) copy-start(s32[2,1,16]{2,1,0:T(1,128)} %param.12) | copy-start | bytes 388
  146.6 20.6 %copy-start = (bf16[1024,3072]{1,0:T(8,128)(2,1)}, bf16[1024,3072]{1,0:T(8,128)(2,1)S(1)}, u32[]{:S(2)}) copy-start(bf16[1024,3072]{1,0:T(8,128)(2,1)S(1)} %convolution_convert_fusion.q_ref.k_ref.v_ref) | copy-start | bytes 18874372
  146.8 20.4 %copy-start.3 = (bf16[2,512,1024]{2,1,0:T(8,128)(2,1)S(1)}, bf16[2,512,1024]{2,1,0:T(8,128)(2,1)}, u32[]{:S(2)}) copy-start(bf16[2,512,1024]{2,1,0:T(8,128)(2,1)} %param.11) | copy-start | bytes 6291460
  146.9 20.4 %copy-start.17 = (bf16[2,2,2,2,2,32,1024]{6,5,4,3,2,1,0:T(8,128)(2,1)S(1)}, bf16[2,2,2,2,2,32,1024]{6,5,4,3,2,1,0:T(8,128)(2,1)}, u32[]{:S(2)}) copy-start(bf16[2,2,2,2,2,32,1024]{6,5,4,3,2,1,0:T(8,128)(2,1)} %get-tuple-element.35) | copy-start | bytes 6291460
  173.7 83.2 %copy-start.18 = (bf16[2,2,2,2,2,32,1024]{6,5,4,3,2,1,0:T(8,128)(2,1)S(1)}, bf16[2,2,2,2,2,32,1024]{6,5,4,3,2,1,0:T(8,128)(2,1)}, u32[]{:S(2)}) copy-start(bf16[2,2,2,2,2,32,1024]{6,5,4,3,2,1,0:T(8,128)(2,1)} %get-tuple-element.35) | copy-start | bytes 6291460
  256.9 33.0 %slice-start.2 = ((s8[6291456]{0:T(1024)(128)(4,1)}), s8[4194304]{0:T(1024)(128)(4,1)S(1)}, s32[]{:S(2)}) async-start(s8[6291456]{0:T(1024)(128)(4,1)} %bitcast.122), calls=%async_computation.2 | async-start | bytes 8388608
  261.0 28.9 %slice-start.3 = ((s8[6291456]{0:T(1024)(128)(4,1)}), s8[2097152]{0:T(1024)(128)(4,1)S(1)}, s32[]{:S(2)}) async-start(s8[6291456]{0:T(1024)(128)(4,1)} %bitcast.122), calls=%async_computation.3 | async-start | bytes 4194304
  289.9 4.8 %copy-start.1 = (bf16[3,1024,1024]{2,1,0:T(8,128)(2,1)}, bf16[3,1024,1024]{2,1,0:T(8,128)(2,1)S(1)}, u32[]{:S(2)}) copy-start(bf16[3,1024,1024]{2,1,0:T(8,128)(2,1)S(1)} %attend_back.1) | copy-start | bytes 18874372
  292.3 2.4 copy-start.4
  294.7 5.7 %copy-start.14 = (f32[1,1024]{1,0:T(1,128)S(1)}, f32[1,1024]{1,0:T(1,128)}, u32[]{:S(2)}) copy-start(f32[1,1024]{1,0:T(1,128)} %get-tuple-element.44) | copy-start | bytes 12292
  294.7 6.4 %copy-start.13 = (f32[1,1024]{1,0:T(1,128)S(1)}, f32[1,1024]{1,0:T(1,128)}, u32[]{:S(2)}) copy-start(f32[1,1024]{1,0:T(1,128)} %get-tuple-element.46) | copy-start | bytes 12292
  294.7 7.1 %copy-start.12 = (f32[1,4096]{1,0:T(1,128)S(1)}, f32[1,4096]{1,0:T(1,128)}, u32[]{:S(2)}) copy-start(f32[1,4096]{1,0:T(1,128)} %get-tuple-element.45) | copy-start | bytes 49156
  302.0 7.0 %slice-start = ((s8[6291456]{0:T(1024)(128)(4,1)}), s8[4194304]{0:T(1024)(128)(4,1)S(1)}, s32[]{:S(2)}) async-start(s8[6291456]{0:T(1024)(128)(4,1)} %bitcast.89), calls=%async_computation | async-start | bytes 8388608
  302.7 6.3 %slice-start.1 = ((s8[6291456]{0:T(1024)(128)(4,1)}), s8[2097152]{0:T(1024)(128)(4,1)S(1)}, s32[]{:S(2)}) async-start(s8[6291456]{0:T(1024)(128)(4,1)} %bitcast.89), calls=%async_computation.1 | async-start | bytes 4194304
  302.7 6.3 %copy-start.8 = (bf16[2,512,1024]{2,1,0:T(8,128)(2,1)S(1)}, bf16[2,512,1024]{2,1,0:T(8,128)(2,1)}, u32[]{:S(2)}) copy-start(bf16[2,512,1024]{2,1,0:T(8,128)(2,1)} %copy-done.7) | copy-start | bytes 6291460
  312.8 3.8 copy-start.16
  320.3 131.3 %copy-start.5 = (bf16[2,512,1024]{2,1,0:T(8,128)(2,1)S(1)}, bf16[2,512,1024]{2,1,0:T(8,128)(2,1)}, u32[]{:S(2)}) copy-start(bf16[2,512,1024]{2,1,0:T(8,128)(2,1)} %param.11) | copy-start | bytes 6291460
  320.3 131.3 %copy-start.6 = (f32[1024,1024]{1,0:T(8,128)S(1)}, f32[1024,1024]{1,0:T(8,128)}, u32[]{:S(2)}) copy-start(f32[1024,1024]{1,0:T(8,128)} %get-tuple-element.39) | copy-start | bytes 12582916
  451.6 4.4 copy-start.11
  451.6 5.0 %copy-start.10 = (f32[32,4096]{1,0:T(8,128)S(1)}, f32[32,4096]{1,0:T(8,128)}, u32[]{:S(2)}) copy-start(f32[32,4096]{1,0:T(8,128)} %get-tuple-element.81) | copy-start | bytes 1572868
  451.6 5.8 %copy-start.9 = (f32[128,1024]{1,0:T(8,128)S(1)}, f32[128,1024]{1,0:T(8,128)}, u32[]{:S(2)}) copy-start(f32[128,1024]{1,0:T(8,128)} %get-tuple-element.83) | copy-start | bytes 1572868

commit v3 on v2

--- a/solution.py
+++ b/solution.py
@@ -64,169 +64,6 @@
             events += [(u + skew * s, s, piece, h) for s in range(steps + 1)]
             piece += 1
     return [(p, s) for _, s, p, _ in sorted(events)]
-
-
-def gather_kernel(table, n, chunks, times, *refs):
-    shards, fulls = refs[:n], refs[n:2 * n]
-    local_sem, send_sem, recv_sem = refs[2 * n:]
-    bits, where = my_bits(table)
-    steps = len(table)
-    greet(table, bits, where)
-
-    def view(c, done):
-        i, rows, cols, _ = chunks[c]
-        index = tuple(slice(None) if k in done else bits[k] for k in range(steps))
-        return fulls[i].at[index + (rows, cols)]
-
-    own, copies = [], {}
-    for i in range(n):
-        index = tuple(bits[k] for k in range(steps))
-        copy = pltpu.make_async_copy(shards[i], fulls[i].at[index], local_sem.at[i])
-        copy.start()
-        own.append(copy)
-    arrived = set()
-    for c, s in times:
-        i, rows, cols, order = chunks[c]
-        if s > 0:
-            copies[c, s - 1].wait_recv()
-            if i not in arrived:
-                arrived.add(i)
-                own[i].wait()
-        if s < steps:
-            there = view(c, order[:s])
-            copy = pltpu.make_async_remote_copy(
-                src_ref=shards[i].at[rows, cols] if s == 0 else there, dst_ref=there,
-                send_sem=send_sem.at[c, s], recv_sem=recv_sem.at[c, s],
-                device_id=partner(table, bits, where, order[s]), device_id_type=pl.DeviceIdType.MESH)
-            copy.start()
-            copies[c, s] = copy
-    for copy in copies.values():
-        copy.wait_send()
-
-
-def gather(shards, sizes, collective_id):
-    table = bit_table(sizes)
-    steps = len(table)
-    two = [o[::-1] for o in orders(table)]
-    units = units_of([a.shape for a in shards])
-    chunks = [piece + (two[(h + u) % 2],) for u, unit in enumerate(units) for h, piece in enumerate(unit)]
-    out = pl.pallas_call(
-        functools.partial(gather_kernel, table, len(shards), chunks, timetable(units, steps, SKEW)),
-        out_shape=[jax.ShapeDtypeStruct((2,) * steps + a.shape, a.dtype) for a in shards],
-        in_specs=[pl.BlockSpec(memory_space=pl.ANY)] * len(shards),
-        out_specs=[pl.BlockSpec(memory_space=pl.ANY)] * len(shards),
-        scratch_shapes=[pltpu.SemaphoreType.DMA((len(shards),)), pltpu.SemaphoreType.DMA((len(chunks), steps)), pltpu.SemaphoreType.DMA((len(chunks), steps))],
-        compiler_params=pltpu.CompilerParams(collective_id=collective_id, has_side_effects=True),
-        name="gather",
-    )(*shards)
-    return [f.reshape((f.shape[-2] * 2 ** steps,) + f.shape[-1:]) for f in out]
-
-
-def scatter_kernel(table, plan, *refs):
-    n, chunks, times, steps = plan["n"], plan["chunks"], plan["times"], len(table)
-    parts, outs = refs[:n], refs[n:2 * n]
-    m = len(chunks)
-    keep = refs[2 * n:2 * n + m]
-    recv = [refs[2 * n + m + c * steps:2 * n + m + (c + 1) * steps] for c in range(m)]
-    local_sem, send_sem, recv_sem = refs[2 * n + m + m * steps:]
-    bits, where = my_bits(table)
-    greet(table, bits, where)
-    copies = {}
-    loads = {}
-
-    def index(order, s, last):
-        out = []
-        for k in range(steps):
-            if k in order[1:s]:
-                out.append(bits[k])
-            elif k == order[0]:
-                continue
-            elif s < steps and k == order[s] and last is not None:
-                out.append(last)
-            else:
-                out.append(slice(None))
-        return tuple(out)
-
-    def start(c, s):
-        i, rows, cols, order = chunks[c]
-        k = order[s]
-        other = 1 - bits[k]
-        if s == 0:
-            full = tuple(other if q == k else slice(None) for q in range(steps))
-            src = parts[i].at[full + (rows, cols)]
-        else:
-            src = keep[c].at[index(order, s, other)]
-        copy = pltpu.make_async_remote_copy(
-            src_ref=src, dst_ref=recv[c][s], send_sem=send_sem.at[c, s], recv_sem=recv_sem.at[c, s],
-            device_id=partner(table, bits, where, k), device_id_type=pl.DeviceIdType.MESH)
-        copy.start()
-        copies[c, s] = copy
-
-    def add(c, s):
-        i, rows, cols, order = chunks[c]
-        left = steps - s - 1
-        if left == 0:
-            own = keep[c][index(order, steps, None)] if steps > 1 else keep[c][...]
-            outs[i][rows, cols] = own.astype(jnp.float32) + recv[c][s][...].astype(jnp.float32)
-            return
-        base = index(order, s, bits[order[s]] if s else None)
-
-        @pl.loop(0, 2 ** left)
-        def _(j):
-            free, at = [], []
-            for b in range(left):
-                free.append((j // 2 ** (left - 1 - b)) % 2)
-            pos = 0
-            for e in base:
-                if isinstance(e, slice):
-                    at.append(free[pos])
-                    pos += 1
-                else:
-                    at.append(e)
-            here = tuple(at)
-            got = recv[c][s][tuple(free)]
-            keep[c][here] = (keep[c][here].astype(jnp.float32) + got.astype(jnp.float32)).astype(keep[c].dtype)
-
-    for c, s in times:
-        i, rows, cols, order = chunks[c]
-        if s == 0:
-            full = tuple(bits[k] if k == order[0] else slice(None) for k in range(steps))
-            loads[c] = pltpu.make_async_copy(parts[i].at[full + (rows, cols)], keep[c], local_sem.at[c])
-            loads[c].start()
-        else:
-            copies[c, s - 1].wait_recv()
-            if s == 1:
-                loads[c].wait()
-            add(c, s - 1)
-        if s < steps:
-            start(c, s)
-    for copy in copies.values():
-        copy.wait_send()
-
-
-def scatter(parts, sizes, collective_id):
-    table = bit_table(sizes)
-    steps = len(table)
-    two = orders(table)
-    owners = 2 ** steps
-    parts = [a.reshape((2,) * steps + (a.shape[0] // owners, a.shape[1])) for a in parts]
-    units = units_of([a.shape[-2:] for a in parts])
-    chunks = [piece + (two[(h + u) % 2],) for u, unit in enumerate(units) for h, piece in enumerate(unit)]
-    keep, recv = [], []
-    for i, rows, cols, order in chunks:
-        tail = (rows.stop - rows.start, cols.stop - cols.start)
-        keep.append(pltpu.VMEM((2,) * (steps - 1) + tail, parts[i].dtype))
-        recv += [pltpu.VMEM((2,) * (steps - 1 - s) + tail, parts[i].dtype) for s in range(steps)]
-    plan = {"n": len(parts), "chunks": chunks, "times": timetable(units, steps, SKEW)}
-    return pl.pallas_call(
-        functools.partial(scatter_kernel, table, plan),
-        out_shape=[jax.ShapeDtypeStruct(a.shape[-2:], jnp.float32) for a in parts],
-        in_specs=[pl.BlockSpec(memory_space=pl.ANY)] * len(parts),
-        out_specs=[pl.BlockSpec(memory_space=pltpu.VMEM)] * len(parts),
-        scratch_shapes=keep + recv + [pltpu.SemaphoreType.DMA((len(chunks),)), pltpu.SemaphoreType.DMA((len(chunks), steps)), pltpu.SemaphoreType.DMA((len(chunks), steps))],
-        compiler_params=pltpu.CompilerParams(collective_id=collective_id, has_side_effects=True, vmem_limit_bytes=56 * 2 ** 20),
-        name="scatter",
-    )(*parts)
 
 
 EPS = 1e-06
@@ -462,28 +299,664 @@
     )(project, project, project, grad, start, logsum)
 
 
-def pack(vectors, owners, rows):
-    flat = jnp.concatenate([v.reshape(owners, -1) for v in vectors], axis=1)
-    return jnp.pad(flat, ((0, 0), (0, rows * 128 - flat.shape[1]))).reshape(owners * rows, 128)
-
-
-def unpack(packed, owners, widths):
-    flat = packed.reshape(owners, -1)
-    out, at = [], 0
-    for w in widths:
-        out.append(flat[:, at:at + w].reshape(-1))
-        at += w
-    return out
+class Gather:
+    def __init__(self, table, bits, where, shards, fulls, local_sem, send_sem, recv_sem):
+        self.table, self.bits, self.steps = table, bits, len(table)
+        self.partners = [partner(table, bits, where, k) for k in range(len(table))]
+        self.shards, self.fulls = shards, fulls
+        self.local_sem, self.send_sem, self.recv_sem = local_sem, send_sem, recv_sem
+        two = [o[::-1] for o in orders(table)]
+        self.units = units_of([s.shape for s in shards])
+        self.chunks = [piece + (two[(h + u) % 2],) for u, unit in enumerate(self.units) for h, piece in enumerate(unit)]
+        self.events = timetable(self.units, self.steps, SKEW)
+        self.at = 0
+        pieces = {i: [e for e in self.events if self.chunks[e[0]][0] == i and e[1] == 1] for i in range(len(shards))}
+        self.first = {found[0] for found in pieces.values()}
+
+    def own(self, i):
+        return pltpu.make_async_copy(self.shards[i], self.fulls[i].at[tuple(self.bits)], self.local_sem.at[i])
+
+    def copy(self, c, s):
+        i, rows, cols, order = self.chunks[c]
+        index = tuple(slice(None) if k in order[:s] else self.bits[k] for k in range(self.steps))
+        there = self.fulls[i].at[index + (rows, cols)]
+        return pltpu.make_async_remote_copy(
+            src_ref=self.shards[i].at[rows, cols] if s == 0 else there, dst_ref=there,
+            send_sem=self.send_sem.at[c, s], recv_sem=self.recv_sem.at[c, s],
+            device_id=self.partners[order[s]], device_id_type=pl.DeviceIdType.MESH)
+
+    def event(self, c, s):
+        i = self.chunks[c][0]
+        if s > 0:
+            self.copy(c, s - 1).wait_recv()
+            if (c, s) in self.first:
+                self.own(i).wait()
+        if s < self.steps:
+            self.copy(c, s).start()
+
+    def run(self, count):
+        for c, s in self.events[self.at:self.at + count]:
+            self.event(c, s)
+        self.at = min(self.at + count, len(self.events))
+
+    def needed(self, array, unit):
+        piece, last = 0, 0
+        seen = -1
+        for u in self.units:
+            seen += u[0][0] == array
+            if u[0][0] == array and seen <= unit:
+                ends = [self.events.index((piece + h, self.steps)) for h in range(len(u))]
+                last = max(last, max(ends) + 1)
+            piece += len(u)
+        return max(0, last - self.at)
+
+    def until(self, array, unit):
+        self.run(self.needed(array, unit))
+
+    def finish(self):
+        self.run(len(self.events))
+        for c in range(len(self.chunks)):
+            for s in range(self.steps):
+                self.copy(c, s).wait_send()
+
+
+def spread(index, slots, engine, count):
+    done = 0
+    for slot in range(slots):
+        upto = count * (slot + 1) // slots
+        if upto > done:
+            pl.when(index == slot)(functools.partial(engine.run, upto - done))
+            done = upto
+
+
+def row_of(table, offset, width, total):
+    owners = table.shape[0]
+    lane = lax.broadcasted_iota(jnp.int32, (128, total), 0)
+    col = lax.broadcasted_iota(jnp.int32, (128, total), 1)
+    pick = jnp.where(lane == offset + col % width, 1.0, 0.0).astype(BF16)
+    owner = lax.broadcasted_iota(jnp.int32, (owners, total), 0)
+    mine = owner == lax.broadcasted_iota(jnp.int32, (owners, total), 1) // width
+    return jnp.sum(jnp.where(mine, mul(table, pick), 0.0), axis=0, keepdims=True)
+
+
+def rows_at(i, size):
+    return pl.ds(pl.multiple_of(i * size, size), size)
+
+
+def norm_rows(x):
+    factor = lax.rsqrt(jnp.mean(x * x, axis=-1, keepdims=True) + EPS)
+    return x * factor, factor
+
+
+def attend_pair(q_ref, k_ref, v_ref, bias, out, logsum):
+    rows, wide = q_ref.shape
+    lanes = lax.broadcasted_iota(jnp.int32, (PIECE, wide), 1) < wide // 2
+    at = 0
+    for i, (low, q, high) in enumerate(spans(rows)):
+        n = high - low
+        queries = side_by_side(q_ref[q:high, :] * 0.125, lanes)
+        scores = mul(k_ref[low:high, :], queries, NT) + bias[at:at + n, :]
+        peak = jnp.max(scores, axis=0, keepdims=True)
+        expo = jnp.exp(scores - peak)
+        total = jnp.sum(expo, axis=0, keepdims=True)
+        logsum[i:i + 1, :] = peak + jnp.log(total)
+        attend_low = (expo * (1.0 / total)).astype(BF16)
+        both = mul(attend_low, v_ref[low:high, :], TN)
+        out[q:high, :] = jnp.where(lanes, both[:PIECE], both[PIECE:]).astype(BF16)
+        at += n
+
+
+def forward_kernel(table, x_ref, cot_hbm, start, small_s, qkv_s, out_s, down_s, up_s,
+                   small, qkv, out_w, down, up, project_o, attended_o, entered_o, output_o, middle_o, branch_o, up_g, down_g,
+                   logsum, first_row, up_b_g, gain_g, down_b_g,
+                   cot, entered, project, attended, middle, total, back, active, grad_hidden, up_v, down_v, up_gv, down_gv, small_v, rows_v, bias_v, bias,
+                   local_sem, send_sem, recv_sem, sems):
+    bits, where = my_bits(table)
+    steps, owners = len(table), 2 ** len(table)
+    rows, width = x_ref.shape
+    ff = up_s.shape[1]
+    length = start.shape[2]
+    pairs = width // 128
+    g = Gather(table, bits, where, [small_s, qkv_s, out_s, down_s, up_s], [small, qkv, out_w, down, up], local_sem, send_sem, recv_sem)
+    SMALL, QKV, OUT, DOWN, UP = range(5)
+    greet(table, bits, where)
+    for i in range(5):
+        g.own(i).start()
+
+    def move(src, dst, k):
+        return pltpu.make_async_copy(src, dst, sems.at[k])
+
+    move(cot_hbm, cot, 0).start()
+    g.until(SMALL, 0)
+    move(small, small_v, 1).start()
+    move(small, small_v, 1).wait()
+    held = small_v[...].reshape(owners, small_s.shape[0], 128)
+    first_row[...] = row_of(held[:, 1], 0, width // owners, width)
+    rows_v[0:1, :] = row_of(held[:, 1], width // owners, width // owners, width)
+    rows_v[1:2, :] = row_of(held[:, 1], 2 * (width // owners), width // owners, width)
+    bias_v[...] = row_of(held[:, 0], 0, ff // owners, ff)
+    part = 128
+
+    @pl.loop(0, rows // part)
+    def _(i):
+        at = rows_at(i, part)
+        normal, _ = norm_rows(x_ref[at, :].astype(F32))
+        entered[at, :] = (normal * first_row[...]).astype(BF16)
+    move(entered, entered_o, 2).start()
+
+    for u in range(3):
+        g.until(QKV, u)
+        fetch = move(qkv.at[(slice(None),) * (steps + 1) + (slice(u * width, (u + 1) * width),)], up_v.at[u % 2], 3)
+        fetch.start()
+        fetch.wait()
+
+        @pl.loop(0, rows // TALL)
+        def _(i):
+            at = rows_at(i, TALL)
+            project[at, u * width:(u + 1) * width] = mul(entered[at, :], up_v[u % 2].reshape(width, width)).astype(BF16)
+            spread_fixed(i, rows // TALL, g, 8)
+        g.at += 8
+    move(project, project_o, 4).start()
+    loops = rows // length * pairs
+    slot_events = 64
+
+    @pl.loop(0, loops)
+    def _(i):
+        b, h = i // pairs, i % pairs
+
+        @pl.when(h == 0)
+        def _():
+            fill_bias(bias, start[b], length)
+        at = rows_at(b, length)
+        lanes = [pl.ds(pl.multiple_of(k * width + h * 128, 128), 128) for k in range(3)]
+        q_ref, k_ref, v_ref = [project.at[at, lane] for lane in lanes]
+        attend_pair(q_ref, k_ref, v_ref, bias, attended.at[at, lanes[0]], logsum.at[b, h])
+        spread_fixed(i, loops, g, slot_events)
+    g.at += slot_events
+    move(attended, attended_o, 5).start()
+    g.until(OUT, 0)
+    fetch = move(out_w, up_v.at[1], 3)
+    fetch.start()
+    fetch.wait()
+    move(entered, entered_o, 2).wait()
+    second = entered
+
+    @pl.loop(0, rows // TALL)
+    def _(i):
+        at = rows_at(i, TALL)
+        x = x_ref[at, :].astype(F32) + mul(attended[at, :], up_v[1].reshape(width, width))
+        middle[at, :] = x
+        normal, _ = norm_rows(x)
+        second[at, :] = (normal * rows_v[0:1, :]).astype(BF16)
+        spread_fixed(i, rows // TALL, g, 8)
+    g.at += 8
+    g.until(UP, 0)
+    move(cot_hbm, cot, 0).wait()
+    blocks = ff // BLOCK
+    lead = blocks.bit_length() - 1
+
+    def fetches(j, slot):
+        top = tuple((j // 2 ** (lead - 1 - k)) % 2 for k in range(lead))
+        return [move(up.at[(slice(None),) * (steps + 1) + (rows_at(j, BLOCK),)], up_v.at[slot], 6 + slot),
+                move(down.at[top], down_v.at[slot], 8 + slot)]
+
+    def stores(j, slot):
+        return [move(up_gv.at[slot], up_g.at[:, rows_at(j, BLOCK)], 10 + slot), move(down_gv.at[slot], down_g.at[rows_at(j, BLOCK), :], 12 + slot)]
+
+    for f in fetches(0, 0):
+        f.start()
+    left = len(g.events) - g.at
+    per = rows // TALL
+
+    @pl.loop(0, blocks)
+    def _(j):
+        slot = j % 2
+        for f in fetches(j, slot):
+            f.wait()
+
+        @pl.when(j >= 2)
+        def _():
+            for f in stores(j, slot):
+                f.wait()
+        lane = rows_at(j, BLOCK)
+        bias_row = bias_v[:, lane]
+        up_b_g[:, lane] = jnp.zeros((1, BLOCK), F32)
+
+        @pl.loop(0, per)
+        def _(i):
+            at = rows_at(i, TALL)
+            hidden = mul(second[at, :], up_v[slot].reshape(width, BLOCK)) + bias_row
+            grad = mul(cot[at, :], down_v[slot].reshape(BLOCK, width), NT)
+            half = 0.5 + 0.5 * lax.erf(hidden * (0.5 ** 0.5))
+            slope = half + hidden * (jnp.exp(hidden * hidden * -0.5) * 0.3989422804014327)
+            active[at, :] = (hidden * half).astype(BF16)
+            low = (grad * slope).astype(BF16)
+            grad_hidden[at, :] = low
+            up_b_g[:, lane] += jnp.sum(low.astype(F32), axis=0, keepdims=True)
+            pl.when(j == 0)(lambda: spread_fixed(i, per, g, left // 2))
+        mark = g.at
+        g.at += left // 2
+
+        @pl.loop(0, per)
+        def _(i):
+            at = rows_at(i, TALL)
+            more, less = mul(active[at, :], down_v[slot].reshape(BLOCK, width)), mul(grad_hidden[at, :], up_v[slot].reshape(width, BLOCK), NT)
+
+            @pl.when(j == 0)
+            def _():
+                total[at, :] = more
+                back[at, :] = less
+                spread_fixed(i, per, g, left - left // 2)
+
+            @pl.when(j > 0)
+            def _():
+                total[at, :] += more
+                back[at, :] += less
+        g.at = mark
+
+        @pl.when(j + 1 < blocks)
+        def _():
+            for f in fetches(j + 1, 1 - slot):
+                f.start()
+
+        @pl.loop(0, BLOCK // TALL)
+        def _(i):
+            at = rows_at(i, TALL)
+            down_gv[slot, at, :] = mul(active[:, at], cot[...], TN).astype(BF16)
+
+        @pl.loop(0, width // TALL)
+        def _(i):
+            at = rows_at(i, TALL)
+            up_gv[slot, at, :] = mul(second[:, at], grad_hidden[...], TN).astype(BF16)
+        for f in stores(j, slot):
+            f.start()
+    g.at += left
+    move(attended, attended_o, 5).wait()
+    output, branch = entered, attended
+    gain_g[...] = jnp.zeros_like(gain_g)
+    down_b_g[...] = jnp.zeros_like(down_b_g)
+
+    @pl.loop(0, rows // part)
+    def _(i):
+        at = rows_at(i, part)
+        x = middle[at, :]
+        normal, factor = norm_rows(x)
+        output[at, :] = (x + (total[at, :] + rows_v[1:2, :])).astype(BF16)
+        c = cot[at, :].astype(F32)
+        grad = back[at, :]
+        gain_g[...] += jnp.sum(grad * normal, axis=0, keepdims=True)
+        down_b_g[...] += jnp.sum(c, axis=0, keepdims=True)
+        n = grad * rows_v[0:1, :]
+        result = c + factor * (n - normal * jnp.mean(n * normal, axis=-1, keepdims=True))
+        back[at, :] = result
+        branch[at, :] = result.astype(BF16)
+    last = [move(output, output_o, 2), move(back, middle_o, 3), move(branch, branch_o, 5)]
+    for f in last:
+        f.start()
+    for f in last + [move(project, project_o, 4)] + stores(blocks - 2, blocks % 2) + stores(blocks - 1, (blocks - 1) % 2):
+        f.wait()
+    g.finish()
+
+
+def spread_fixed(index, slots, engine, count):
+    begin = engine.at
+    spread(index, slots, engine, count)
+    engine.at = begin
+
+
+def forward(frames, cot, start, packed, qkv, out, down, up, sizes, collective_id):
+    table = bit_table(sizes)
+    steps, owners = len(table), 2 ** len(table)
+    rows, width = frames.shape
+    ff = up.shape[1]
+    batches, length = start.shape[0], start.shape[2]
+    pairs = width // 128
+    two = (2,) * steps
+    shards = [packed, qkv, out, down, up]
+    pieces = sum(len(u) for u in units_of([a.shape for a in shards]))
+    anywhere, vmem = pl.BlockSpec(memory_space=pl.ANY), pl.BlockSpec(memory_space=pltpu.VMEM)
+    hbm_out = [(two + a.shape, BF16) for a in shards] + [((rows, 3 * width), BF16), ((rows, width), BF16), ((rows, width), BF16),
+               ((rows, width), BF16), ((rows, width), F32), ((rows, width), BF16), ((width, ff), BF16), ((ff, width), BF16)]
+    vmem_out = [((batches, pairs, length // PIECE, 2 * PIECE), F32), ((1, width), F32), ((1, ff), F32), ((1, width), F32), ((1, width), F32)]
+    lead = (ff // BLOCK).bit_length() - 1
+    V = pltpu.VMEM
+    return pl.pallas_call(
+        functools.partial(forward_kernel, table),
+        out_shape=[jax.ShapeDtypeStruct(s, d) for s, d in hbm_out + vmem_out],
+        in_specs=[vmem, anywhere, vmem] + [anywhere] * 5,
+        out_specs=[anywhere] * len(hbm_out) + [vmem] * len(vmem_out),
+        scratch_shapes=[V((rows, width), BF16), V((rows, width), BF16), V((rows, 3 * width), BF16), V((rows, width), BF16), V((rows, width), F32),
+                        V((rows, width), F32), V((rows, width), F32), V((rows, BLOCK), BF16), V((rows, BLOCK), BF16),
+                        V((2,) + two + (width // owners, BLOCK), BF16), V((2,) + two[lead:] + (ff // owners, width), BF16),
+                        V((2, width, BLOCK), BF16), V((2, BLOCK, width), BF16), V(two + packed.shape, BF16), V((2, width), F32), V((1, ff), F32),
+                        V((sum(h - l for l, _, h in spans(length)), 2 * PIECE), F32),
+                        pltpu.SemaphoreType.DMA((5,)), pltpu.SemaphoreType.DMA((pieces, steps)), pltpu.SemaphoreType.DMA((pieces, steps)),
+                        pltpu.SemaphoreType.DMA((14,))],
+        compiler_params=pltpu.CompilerParams(collective_id=collective_id, has_side_effects=True, vmem_limit_bytes=58 * 2 ** 20),
+        name="forward",
+    )(frames, cot, start, *shards)
+
+
+class Scatter:
+    def __init__(self, table, bits, where, parts, outs, recv, stage, small, local_sem, send_sem, recv_sem):
+        self.table, self.bits, self.steps = table, bits, len(table)
+        self.partners = [partner(table, bits, where, k) for k in range(len(table))]
+        self.parts, self.outs, self.recv, self.stage = parts, outs, recv, stage
+        self.local_sem, self.send_sem, self.recv_sem = local_sem, send_sem, recv_sem
+        self.small_recv = small
+        self.units, self.chunks = scatter_chunks(table, [p.shape[-2:] for p in parts])
+        self.events = timetable(self.units, self.steps, SKEW)
+        self.at = 0
+
+    def into(self, c, s):
+        if self.chunks[c][0] == len(self.parts) - 1:
+            return self.small_recv[s]
+        return self.recv[s].at[c]
+
+    def half(self, c, bit):
+        i, rows, cols, order = self.chunks[c]
+        index = tuple(bit if k == order[0] else slice(None) for k in range(self.steps))
+        return self.parts[i].at[index + (rows, cols)]
+
+    def load(self, c):
+        return pltpu.make_async_copy(self.half(c, self.bits[self.chunks[c][3][0]]), self.stage.at[c % 4], self.local_sem.at[c % 4])
+
+    def left(self, c, s, last):
+        order, out = self.chunks[c][3], []
+        for k in range(self.steps):
+            if k == order[0]:
+                continue
+            if k in order[1:s]:
+                out.append(self.bits[k])
+            elif s < self.steps and k == order[s] and last is not None:
+                out.append(last)
+            else:
+                out.append(slice(None))
+        return tuple(out)
+
+    def copy(self, c, s):
+        k = self.chunks[c][3][s]
+        other = 1 - self.bits[k]
+        return pltpu.make_async_remote_copy(
+            src_ref=self.half(c, other) if s == 0 else self.into(c, 0).at[self.left(c, s, other)], dst_ref=self.into(c, s),
+            send_sem=self.send_sem.at[c, s], recv_sem=self.recv_sem.at[c, s],
+            device_id=self.partners[k], device_id_type=pl.DeviceIdType.MESH)
+
+    def add(self, c, s):
+        i, rows, cols, order = self.chunks[c]
+        small = i == len(self.parts) - 1
+        total, got = self.into(c, 0), self.into(c, s)
+        free = self.steps - s - 1
+        if free == 0:
+            own = total[self.left(c, self.steps, None)]
+            self.outs[i][rows, cols] = own.astype(F32) + got[...].astype(F32)
+            return
+        base = self.left(c, s, self.bits[order[s]]) if s else (slice(None),) * free
+        mine = self.half(c, self.bits[order[0]]) if small else self.stage.at[c % 4]
+
+        @pl.loop(0, 2 ** free)
+        def _(j):
+            spot = [(j // 2 ** (free - 1 - b)) % 2 for b in range(free)]
+            rest = iter(spot)
+            here = tuple(next(rest) if isinstance(e, slice) else e for e in base)
+            more = mine[tuple(spot)] if s == 0 else got[tuple(spot)]
+            total[here] = (total[here].astype(F32) + more.astype(F32)).astype(total.dtype)
+
+    def event(self, c, s):
+        small = self.chunks[c][0] == len(self.parts) - 1
+        if s == 0:
+            self.copy(c, 0).start()
+            if not small:
+                self.load(c).start()
+            return
+        self.copy(c, s - 1).wait_recv()
+        if s == 1 and not small:
+            self.load(c).wait()
+        self.add(c, s - 1)
+        if s < self.steps:
+            self.copy(c, s).start()
+
+    def run(self, count):
+        for c, s in self.events[self.at:self.at + count]:
+            self.event(c, s)
+        self.at = min(self.at + count, len(self.events))
+
+    def before(self, part):
+        return next(n for n, (c, s) in enumerate(self.events) if self.chunks[c][0] == part)
+
+    def finish(self):
+        self.run(len(self.events))
+        for c in range(len(self.chunks)):
+            for s in range(self.steps):
+                self.copy(c, s).wait_send()
+
+
+def scatter_chunks(table, tails):
+    two = orders(table)
+    units = units_of(tails)
+    return units, [piece + (two[(h + u) % 2],) for u, unit in enumerate(units) for h, piece in enumerate(unit)]
+
+
+def attend_back_pair(q_ref, k_ref, v_ref, g_ref, bias, logsum, k_sum, v_sum):
+    rows, wide = q_ref.shape
+    lanes = lax.broadcasted_iota(jnp.int32, (PIECE, wide), 1) < wide // 2
+    at = 0
+    k_sum[...] = jnp.zeros_like(k_sum)
+    v_sum[...] = jnp.zeros_like(v_sum)
+    for i, (low, q, high) in enumerate(spans(rows)):
+        n = high - low
+        queries = side_by_side(q_ref[q:high, :] * 0.125, lanes)
+        grads = side_by_side(g_ref[q:high, :], lanes)
+        keys, values = k_ref[low:high, :], v_ref[low:high, :]
+        scores = mul(keys, queries, NT) + bias[at:at + n, :]
+        full = jnp.exp(scores - logsum[i:i + 1, :])
+        grad = mul(values, grads, NT)
+        v_sum[low:high, :] += mul(full.astype(BF16), grads)
+        total = jnp.sum(full * grad, axis=0, keepdims=True)
+        grad_scores = (full * (grad - total)).astype(BF16)
+        k_sum[low:high, :] += mul(grad_scores, queries)
+        both = mul(grad_scores, keys, TN) * 0.125
+        q_ref[q:high, :] = jnp.where(lanes, both[:PIECE], both[PIECE:]).astype(BF16)
+        at += n
+    k_ref[...] = k_sum[...].astype(BF16)
+    v_ref[...] = v_sum[...].astype(BF16)
+
+
+def by_owner(row, offset, owners):
+    total = row.shape[1]
+    width = total // owners
+    lane = lax.broadcasted_iota(jnp.int32, (128, total), 0)
+    col = lax.broadcasted_iota(jnp.int32, (128, total), 1)
+    pick = jnp.where(lane == offset + col % width, 1.0, 0.0)
+    owner = lax.broadcasted_iota(jnp.int32, (owners, total), 0)
+    mine = owner == lax.broadcasted_iota(jnp.int32, (owners, total), 1) // width
+    return lax.dot_general(jnp.where(mine, row, 0.0), pick, NT, precision=lax.Precision.HIGHEST, preferred_element_type=F32)
+
+
+def backward_kernel(table, x_hbm, start, project_hbm, attended_hbm, entered_hbm, middle_hbm, branch_hbm, qkv, out_w, up_g, down_g,
+                    logsum, first_row, up_b_g, gain_g, down_b_g,
+                    grad_o, out_g, q_g, k_g, v_g, up_r, down_r, out_r, q_r, k_r, v_r, small_r,
+                    project, attended, branch, entered, weight, held, back, old, bias, k_sum, v_sum, small, stage,
+                    r0, r1, r2, r3, r4, s0, s1, s2, s3, s4, local_sem, send_sem, recv_sem, sems):
+    bits, where = my_bits(table)
+    steps, owners = len(table), 2 ** len(table)
+    rows, width = attended.shape
+    length = start.shape[2]
+    pairs = width // 128
+    e = Scatter(table, bits, where, [up_g, down_g, out_g, q_g, k_g, v_g, small], [up_r, down_r, out_r, q_r, k_r, v_r, small_r],
+                [r0, r1, r2, r3, r4], stage, [s0, s1, s2, s3, s4], local_sem, send_sem, recv_sem)
+
+    def move(src, dst, k):
+        return pltpu.make_async_copy(src, dst, sems.at[k])
+
+    for args in ((attended_hbm, attended, 0), (branch_hbm, branch, 1), (out_w, weight.at[0], 2), (project_hbm, project, 3), (entered_hbm, entered, 4)):
+        move(*args).start()
+    greet(table, bits, where)
+    first_q = e.before(3)
+    e.run(2)
+    move(attended_hbm, attended, 0).wait()
+    move(branch_hbm, branch, 1).wait()
+    per = rows // TALL
+    deep = (width // TALL).bit_length() - 1
+
+    def place(slot, i):
+        return held.at[(slot,) + tuple((i // 2 ** (deep - 1 - k)) % 2 for k in range(deep))]
+
+    def put(slot, i, value):
+        ref = place(slot, i)
+        ref[...] = value.reshape(ref.shape).astype(BF16)
+
+    @pl.loop(0, width // TALL)
+    def _(i):
+        put(0, i, mul(attended[:, rows_at(i, TALL)], branch[...], TN))
+        spread_fixed(i, width // TALL, e, 4)
+    e.at += 4
+    move(held.at[0], out_g, 5).start()
+    move(out_w, weight.at[0], 2).wait()
+
+    @pl.loop(0, per)
+    def _(i):
+        at = rows_at(i, TALL)
+        branch[at, :] = mul(branch[at, :], weight[0].reshape(width, width), NT).astype(BF16)
+        spread_fixed(i, per, e, 4)
+    e.at += 4
+    move(x_hbm, attended, 0).start()
+    move(project_hbm, project, 3).wait()
+    move(held.at[0], out_g, 5).wait()
+    loops = rows // length * pairs
+    count = first_q - e.at - 12
+
+    @pl.loop(0, loops)
+    def _(i):
+        b, h = i // pairs, i % pairs
+
+        @pl.when(h == 0)
+        def _():
+            fill_bias(bias, start[b], length)
+        at = rows_at(b, length)
+        lanes = [pl.ds(pl.multiple_of(k * width + h * 128, 128), 128) for k in range(3)]
+        q_ref, k_ref, v_ref = [project.at[at, lane] for lane in lanes]
+        attend_back_pair(q_ref, k_ref, v_ref, branch.at[at, lanes[0]], bias, logsum.at[b, h], k_sum, v_sum)
+        spread_fixed(i, loops, e, count)
+    e.at += count
+    move(entered_hbm, entered, 4).wait()
+
+    def fetch(u):
+        return move(qkv.at[(slice(None),) * (steps + 1) + (slice(u * width, (u + 1) * width),)], weight.at[(u + 1) % 2], 6 + u % 2)
+
+    fetch(0).start()
+    fetch(1).start()
+    for u, part in enumerate((q_g, k_g, v_g)):
+        slot = (u + 1) % 2
+        if u == 2:
+            move(held.at[slot], q_g, 8).wait()
+
+        @pl.loop(0, width // TALL)
+        def _(i):
+            put(slot, i, mul(entered[:, rows_at(i, TALL)], project[:, u * width:(u + 1) * width], TN))
+            spread_fixed(i, width // TALL, e, 4)
+        e.at += 4
+        move(held.at[slot], part, 8 + u).start()
+    for u, part in enumerate((q_g, k_g, v_g)):
+        if u:
+            move(held.at[(u + 1) % 2], part, 8 + u).wait()
+    mark = e.before(6)
+    each = (mark - e.at) // 3
+    for u in range(3):
+        fetch(u).wait()
+
+        @pl.loop(0, per)
+        def _(i):
+            at = rows_at(i, TALL)
+            more = mul(project[at, u * width:(u + 1) * width], weight[(u + 1) % 2].reshape(width, width), NT)
+            if u == 0:
+                back[at, :] = more
+            else:
+                back[at, :] += more
+            spread_fixed(i, per, e, each)
+        e.at += each
+        if u == 0:
+            fetch(2).start()
+    move(x_hbm, attended, 0).wait()
+    part = old.shape[1]
+    first_g = jnp.zeros((1, width), F32)
+
+    def older(i):
+        return move(middle_hbm.at[rows_at(i, part), :], old.at[i % 2], 11 + i % 2)
+
+    older(0).start()
+
+    @pl.loop(0, rows // part, init_carry=first_g)
+    def first_g(i, first_g):
+        @pl.when(i + 1 < rows // part)
+        def _():
+            older(i + 1).start()
+        older(i).wait()
+        at = rows_at(i, part)
+        normal, factor = norm_rows(attended[at, :].astype(F32))
+        grad = back[at, :]
+        n = grad * first_row[...]
+        back[at, :] = old[i % 2] + factor * (n - normal * jnp.mean(n * normal, axis=-1, keepdims=True))
+        return first_g + jnp.sum(grad * normal, axis=0, keepdims=True)
+    move(back, grad_o, 13).start()
+    share = width // owners
+    zero = jnp.zeros((owners, 6, 128), F32)
+    vectors = by_owner(first_g, 0, owners) + by_owner(gain_g[...], share, owners) + by_owner(down_b_g[...], 2 * share, owners)
+    packed = jnp.concatenate([by_owner(up_b_g[...], 0, owners)[:, None], vectors[:, None], zero], axis=1)
+    small[...] = packed.reshape(small.shape)
+    e.finish()
+    move(back, grad_o, 13).wait()
+
+
+def backward(frames, start, project, attended, entered, middle, branch, qkv, out_w, up_g, down_g, logsum, first_row, up_b_g, gain_g, down_b_g,
+             sizes, collective_id):
+    table = bit_table(sizes)
+    steps, owners = len(table), 2 ** len(table)
+    rows, width = frames.shape
+    length = start.shape[2]
+    two = (2,) * steps
+    share = width // owners
+    up_g = up_g.reshape(two + (share, up_g.shape[1]))
+    down_g = down_g.reshape(two + (down_g.shape[0] // owners, width))
+    small = (8, 128)
+    tails = [up_g.shape[-2:], down_g.shape[-2:]] + [(share, width)] * 4 + [small]
+    units, chunks = scatter_chunks(table, tails)
+    m = len(chunks)
+    piece = (min(ROWS, share), WIDE)
+    anywhere, vmem = pl.BlockSpec(memory_space=pl.ANY), pl.BlockSpec(memory_space=pltpu.VMEM)
+    V = pltpu.VMEM
+    out_shape = [((rows, width), F32)] + [(two + (share, width), BF16)] * 4 + [(t, F32) for t in tails]
+    return pl.pallas_call(
+        functools.partial(backward_kernel, table),
+        out_shape=[jax.ShapeDtypeStruct(s, d) for s, d in out_shape],
+        in_specs=[anywhere, vmem] + [anywhere] * 9 + [vmem] * 5,
+        out_specs=[anywhere] * 5 + [vmem] * 7,
+        scratch_shapes=[V((rows, 3 * width), BF16), V((rows, width), BF16), V((rows, width), BF16), V((rows, width), BF16),
+                        V((2,) + two + (share, width), BF16), V((2,) + two + (share, width), BF16), V((rows, width), F32), V((2, 128, width), F32),
+                        V((sum(h - l for l, _, h in spans(length)), 2 * PIECE), F32), V((length, 128), F32), V((length, 128), F32),
+                        V(two + small, F32), V((4,) + two[1:] + piece, BF16)]
+        + [V((m - 1,) + two[s + 1:] + piece, BF16) for s in range(steps)] + [V(two[s + 1:] + small, F32) for s in range(steps)]
+        + [pltpu.SemaphoreType.DMA((4,)), pltpu.SemaphoreType.DMA((m, steps)), pltpu.SemaphoreType.DMA((m, steps)), pltpu.SemaphoreType.DMA((14,))],
+        compiler_params=pltpu.CompilerParams(collective_id=collective_id, has_side_effects=True, vmem_limit_bytes=60 * 2 ** 20),
+        name="backward",
+    )(frames, start, project, attended, entered, middle, branch, qkv, out_w, up_g, down_g, logsum, first_row, up_b_g, gain_g, down_b_g)
+
+
+def pack(first, second, up_b, down_b):
+    rest = jnp.concatenate([first, second, down_b])
+    rest = jnp.pad(rest, (0, 128 - rest.shape[0]))
+    return jnp.pad(jnp.stack([jnp.pad(up_b, (0, 128 - up_b.shape[0])), rest]), ((0, 14), (0, 0)))
 
 
 def fits(sizes, shards):
-    return all(s & (s - 1) == 0 for s in sizes.values()) and all(a.shape[0] % 16 == 0 for a in shards)
-
-
-def item_ends(lengths):
+    return all(s & (s - 1) == 0 for s in sizes.values()) and all(a.shape[0] % ROWS == 0 for a in shards)
+
+
+def item_starts(lengths, rows):
     slots = jnp.arange(lengths.shape[1], dtype=jnp.int32)
     ends = jnp.sum(jnp.where(slots[None, :, None] <= slots[None, None, :], lengths[:, :, None], 0), axis=1)
-    return ends
+    position = jnp.arange(rows, dtype=jnp.int32)[None, None, :]
+    return jnp.max(jnp.where(ends[:, :, None] <= position, ends[:, :, None], 0), axis=1, keepdims=True)
 
 
 def normalize(x_val):
@@ -503,9 +976,7 @@
     batches, rows, width = frames.shape
     x_val = frames.reshape(batches * rows, width).astype(F32)
     cot = cotangent.reshape(batches * rows, width)
-    ends = item_ends(lengths)
-    position = jnp.arange(rows, dtype=jnp.int32)[None, None, :]
-    start = jnp.max(jnp.where(ends[:, :, None] <= position, ends[:, :, None], 0), axis=1, keepdims=True)
+    start = item_starts(lengths, rows)
     normal, factor = normalize(x_val)
     gain = first.astype(F32)
     entered = (normal * gain).astype(BF16)
@@ -525,24 +996,28 @@
 
 
 def body(sizes, frames, lengths, cotangent, *shards):
-    owners = sizes["dp"] * sizes["fsdp"]
     weights = [shards[i] for i in (1, 2, 4, 6)]
     vectors = [shards[i] for i in (0, 3, 5, 7)]
-    widths = [v.shape[0] for v in vectors]
-    own_kernels = fits(sizes, weights)
-    if own_kernels:
-        packed, qkv, out, up, down = gather([pack(vectors, 1, 16)] + weights, sizes, 1)
-        first, second, up_b, down_b = unpack(packed, owners, widths)
+    shape = frames.shape
+    if fits(sizes, weights):
+        qkv_s, out_s, up_s, down_s = weights
+        flat = (shape[0] * shape[1], shape[2])
+        x_val, cot = frames.reshape(flat), cotangent.reshape(flat)
+        start = item_starts(lengths[:, 0], shape[1])
+        (_, qkv, out, _, _, project, attended, entered, output, middle, branch, up_g, down_g, logsum, first, up_b_g, second_g, down_b_g) = forward(
+            x_val, cot, start, pack(*vectors), qkv_s, out_s, down_s, up_s, sizes, 1)
+        frames_grad, _, _, _, _, up_g, down_g, out_g, q_g, k_g, v_g, small = backward(
+            x_val, start, project, attended, entered, middle, branch, qkv, out, up_g, down_g, logsum, first, up_b_g, second_g, down_b_g, sizes, 2)
+        output, frames_grad = output.reshape(shape), frames_grad.reshape(shape)
+        share = vectors[0].shape[0]
+        first_g, second_g, down_b_g = [small[1, k * share:(k + 1) * share] for k in range(3)]
+        up_b_g, qkv_g = small[0, :vectors[2].shape[0]], [q_g, k_g, v_g]
     else:
         qkv, out, up, down = [lax.all_gather(w, AXES, axis=0, tiled=True) for w in weights]
         first, second, up_b, down_b = [lax.all_gather(v, AXES, axis=0, tiled=True) for v in vectors]
-    params = (first, qkv, out, second, up, up_b, down, down_b)
-    output, frames_grad, big, small = block_pass(frames, lengths[:, 0], cotangent, params, BF16 if own_kernels else F32)
-    if own_kernels:
-        down_g, up_g, out_g, *qkv_g, packed = scatter([g.astype(BF16) for g in big] + [pack(small, owners, 8)], sizes, 2)
-        first_g, second_g, up_b_g, down_b_g = unpack(packed, 1, widths)
-    else:
-        down_g, up_g, out_g, *qkv_g = [lax.psum_scatter(g.astype(F32), AXES, scatter_dimension=0, tiled=True) for g in big]
+        params = (first, qkv, out, second, up, up_b, down, down_b)
+        output, frames_grad, big, small = block_pass(frames, lengths[:, 0], cotangent, params, F32)
+        down_g, up_g, out_g, *qkv_g = [lax.psum_scatter(g, AXES, scatter_dimension=0, tiled=True) for g in big]
         first_g, second_g, up_b_g, down_b_g = [lax.psum_scatter(g, AXES, scatter_dimension=0, tiled=True) for g in small]
     return (output, frames_grad, first_g, jnp.concatenate(qkv_g, axis=1), out_g, second_g, up_g, up_b_g, down_g, down_b_g)
 

time: 459 us -> 362 us (0.79)
  matrix products: 46.4 us -> 0 us
  Pallas kernels: 390 us -> 345 us
  other arithmetic: 12.7 us -> 4.7 us
    dot_general x10 -> x0, matrix products: 46.4 us -> none  [mul(): return lax.dot_general(a, b, dims, preferred_element_type=F32)]
    pallas_call x5 -> x2, Pallas kernels: 390 us -> 345 us  [the longest x1 209 us: forward(): pl.pallas_call(functools.partial(forward_kernel, table), out_shape=[jax.S...]
where the time goes in v3:
time: 362 us; the launch traced here: 361 us
  Pallas kernels  345 us (95%)
  local copies, waits for them, and re-layouts  10.4 us (3%)
  other arithmetic  4.7 us (1%)
    pallas_call x1, Pallas kernels, forward(): pl.pallas_call(functools.partial(forward_kernel, table), out_shape=[jax.S...  209 us
    pallas_call x1, Pallas kernels, backward(): pl.pallas_call(functools.partial(backward_kernel, table), out_shape=[jax....  136 us

profile of v3, /device:TPU:0, one launch (start us, length us, event | category | flops | bytes accessed | tf_op | source)
XLA Modules:
  0.0 360.9 jit_solution(5705154315368672934)
XLA Ops:
  0.6 0.8 fusion.3
  1.4 0.8 select_reduce_fusion.1
  2.2 0.1 select_reduce_fusion
  2.3 0.6 broadcast_in_dim.45.start
  2.9 1.3 fusion.2.small_s
  4.1 209.2 %forward.1 = (bf16[2,2,2,2,2,16,128]{6,5,4,3,2,1,0:T(8,128)(2,1)}, bf16[2,2,2,2,2,32,3072]{6,5,4,3,2,1,0:T(8,128)(2,1)}, bf16[2,2,2,2,2,32,1024]{6,5,4,3,2,1,0:T...) custom-call(bf16[1024,1024]{1,0:T(8,128)(2,1)} %bitcast.18, ...), custom_call_target="tpu_custom_call" | custom-call | tf_op jit(solution)/shard_map/forward/pallas_call | solution.py:623
  213.3 0.0 copy-start.1
  213.3 136.0 %backward.1 = (f32[1024,1024]{1,0:T(8,128)}, bf16[2,2,2,2,2,32,1024]{6,5,4,3,2,1,0:T(8,128)(2,1)}, bf16[2,2,2,2,2,32,1024]{6,5,4,3,2,1,0:T(8,128)(2,1)}, bf16[2,...) custom-call(bf16[1024,1024]{1,0:T(8,128)(2,1)} %bitcast.19, ...), custom_call_target="tpu_custom_call" | custom-call | tf_op jit(solution)/shard_map/backward/pallas_call | solution.py:929
  349.3 1.2 slice_bitcast_fusion.1
  350.5 1.4 slice_bitcast_fusion
  351.9 1.8 pad_maximum_fusion
  353.7 0.0 copy-done.1
  353.7 0.0 copy-start
  353.7 1.3 copy.26
  355.0 1.6 copy-done
  356.7 0.0 copy-start.4
  356.7 0.0 copy-start.3
  356.7 0.0 copy-start.2
  356.7 2.0 copy.27
  358.7 0.0 copy-done.4
  358.7 0.7 copy.28
  359.3 0.0 copy-done.3
  359.3 0.8 copy.29
  360.1 0.0 copy-done.2
  360.1 0.8 copy.30
  (1 shorter events, 0.0 us)
Async XLA Ops:
  213.3 140.4 %copy-start.1 = (bf16[1024,1024]{1,0:T(8,128)(2,1)S(1)}, bf16[1024,1024]{1,0:T(8,128)(2,1)}, u32[]{:S(2)}) copy-start(bf16[1024,1024]{1,0:T(8,128)(2,1)} %get-tuple-element.33) | copy-start | bytes 6291460
  353.7 2.9 copy-start
  356.7 2.0 copy-start.4
  356.7 2.7 copy-start.3
  356.7 3.5 copy-start.2

commit v4 on v3

--- a/solution.py
+++ b/solution.py
@@ -306,7 +306,7 @@
         self.shards, self.fulls = shards, fulls
         self.local_sem, self.send_sem, self.recv_sem = local_sem, send_sem, recv_sem
         two = [o[::-1] for o in orders(table)]
-        self.units = units_of([s.shape for s in shards])
+        self.units = in_turn(units_of([s.shape for s in shards]), len(shards) - 2)
         self.chunks = [piece + (two[(h + u) % 2],) for u, unit in enumerate(self.units) for h, piece in enumerate(unit)]
         self.events = timetable(self.units, self.steps, SKEW)
         self.at = 0
@@ -335,9 +335,12 @@
             self.copy(c, s).start()
 
     def run(self, count):
-        for c, s in self.events[self.at:self.at + count]:
+        self.some(self.at, self.at + count)
+        self.at = min(self.at + count, len(self.events))
+
+    def some(self, low, high):
+        for c, s in self.events[low:high]:
             self.event(c, s)
-        self.at = min(self.at + count, len(self.events))
 
     def needed(self, array, unit):
         piece, last = 0, 0
@@ -358,6 +361,29 @@
         for c in range(len(self.chunks)):
             for s in range(self.steps):
                 self.copy(c, s).wait_send()
+
+
+def in_turn(units, first):
+    one, two = [u for u in units if u[0][0] == first], [u for u in units if u[0][0] == first + 1]
+    return [u for u in units if u[0][0] < first] + [u for pair in zip(one, two) for u in pair] + [u for u in units if u[0][0] > first + 1]
+
+
+def regroup(src, dst, inward):
+    width = src.shape[1]
+    groups = 128 // ROWS
+    part = lax.broadcasted_iota(jnp.int32, (src.shape[0], 128), 1) // ROWS
+    tiles = width // 128 // groups
+    for k in range(tiles):
+        near = [slice((groups * k + m) * 128, (groups * k + m + 1) * 128) for m in range(groups)]
+        far = [slice((m * tiles + k) * 128, (m * tiles + k + 1) * 128) for m in range(groups)]
+        source, target = (near, far) if inward else (far, near)
+        loaded = [src[:, c].astype(F32) for c in source]
+        for a in range(groups):
+            tile = loaded[a]
+            for b in range(groups):
+                turned = loaded[b] if a == b else pltpu.roll(loaded[b], (b - a) * ROWS % 128, 1)
+                tile = jnp.where(part == b, turned, tile)
+            dst[:, target[a]] = tile.astype(dst.dtype)
 
 
 def spread(index, slots, engine, count):
@@ -406,15 +432,16 @@
         at += n
 
 
-def forward_kernel(table, x_ref, cot_hbm, start, small_s, qkv_s, out_s, down_s, up_s,
+def forward_kernel(table, x_ref, cot_hbm, start, small_s, qkv_s, out_s, down_s, up_as_is,
                    small, qkv, out_w, down, up, project_o, attended_o, entered_o, output_o, middle_o, branch_o, up_g, down_g,
                    logsum, first_row, up_b_g, gain_g, down_b_g,
-                   cot, entered, project, attended, middle, total, back, active, grad_hidden, up_v, down_v, up_gv, down_gv, small_v, rows_v, bias_v, bias,
+                   up_s, cot, entered, project, attended, middle, total, back, active, grad_hidden, up_v, down_v, up_gv, down_gv, small_v, rows_v, bias_v, bias,
                    local_sem, send_sem, recv_sem, sems):
     bits, where = my_bits(table)
     steps, owners = len(table), 2 ** len(table)
     rows, width = x_ref.shape
     ff = up_s.shape[1]
+    regroup(up_as_is, up_s, True)
     length = start.shape[2]
     pairs = width // 128
     g = Gather(table, bits, where, [small_s, qkv_s, out_s, down_s, up_s], [small, qkv, out_w, down, up], local_sem, send_sem, recv_sem)
@@ -434,7 +461,9 @@
     first_row[...] = row_of(held[:, 1], 0, width // owners, width)
     rows_v[0:1, :] = row_of(held[:, 1], width // owners, width // owners, width)
     rows_v[1:2, :] = row_of(held[:, 1], 2 * (width // owners), width // owners, width)
-    bias_v[...] = row_of(held[:, 0], 0, ff // owners, ff)
+    blocks = ff // BLOCK
+    for j in range(blocks):
+        bias_v[:, j * BLOCK:(j + 1) * BLOCK] = row_of(held[:, 0], j * ROWS, ROWS, BLOCK)
     part = 128
 
     @pl.loop(0, rows // part)
@@ -458,7 +487,7 @@
         g.at += 8
     move(project, project_o, 4).start()
     loops = rows // length * pairs
-    slot_events = 64
+    slot_events = max(0, g.needed(UP, 0) - 8)
 
     @pl.loop(0, loops)
     def _(i):
@@ -492,21 +521,36 @@
     g.at += 8
     g.until(UP, 0)
     move(cot_hbm, cot, 0).wait()
-    blocks = ff // BLOCK
-    lead = blocks.bit_length() - 1
+
+    def block(up_ref, down_ref, j):
+        every = (slice(None),) * steps
+        return up_ref.at[every + (slice(None), rows_at(j, BLOCK))], down_ref.at[every + (rows_at(j, ROWS),)]
 
     def fetches(j, slot):
-        top = tuple((j // 2 ** (lead - 1 - k)) % 2 for k in range(lead))
-        return [move(up.at[(slice(None),) * (steps + 1) + (rows_at(j, BLOCK),)], up_v.at[slot], 6 + slot),
-                move(down.at[top], down_v.at[slot], 8 + slot)]
+        one, other = block(up, down, j)
+        return [move(one, up_v.at[slot], 6 + slot), move(other, down_v.at[slot], 8 + slot)]
 
     def stores(j, slot):
-        return [move(up_gv.at[slot], up_g.at[:, rows_at(j, BLOCK)], 10 + slot), move(down_gv.at[slot], down_g.at[rows_at(j, BLOCK), :], 12 + slot)]
+        one, other = block(up_g, down_g, j)
+        return [move(up_gv.at[slot], one, 10 + slot), move(down_gv.at[slot], other, 12 + slot)]
+
+    deep = (BLOCK // TALL).bit_length() - 1
+
+    def put(ref, slot, i, value):
+        there = ref.at[(slot,) + tuple((i // 2 ** (deep - 1 - k)) % 2 for k in range(deep))]
+        there[...] = value.reshape(there.shape).astype(BF16)
 
     for f in fetches(0, 0):
         f.start()
-    left = len(g.events) - g.at
     per = rows // TALL
+    marks = [g.at] + [g.at + g.needed(UP, j + 1) for j in range(blocks - 1)]
+
+    def between(j, i, loop, loops):
+        for k in range(blocks - 1):
+            for n in range(per):
+                cut = [marks[k] + (marks[k + 1] - marks[k]) * (loop * per + n + e) // (loops * per) for e in (0, 1)]
+                if cut[1] > cut[0]:
+                    pl.when(jnp.logical_and(j == k, i == n))(functools.partial(g.some, *cut))
 
     @pl.loop(0, blocks)
     def _(j):
@@ -533,9 +577,7 @@
             low = (grad * slope).astype(BF16)
             grad_hidden[at, :] = low
             up_b_g[:, lane] += jnp.sum(low.astype(F32), axis=0, keepdims=True)
-            pl.when(j == 0)(lambda: spread_fixed(i, per, g, left // 2))
-        mark = g.at
-        g.at += left // 2
+            between(j, i, 0, 3)
 
         @pl.loop(0, per)
         def _(i):
@@ -546,31 +588,31 @@
             def _():
                 total[at, :] = more
                 back[at, :] = less
-                spread_fixed(i, per, g, left - left // 2)
 
             @pl.when(j > 0)
             def _():
                 total[at, :] += more
                 back[at, :] += less
-        g.at = mark
+            between(j, i, 1, 3)
+
+        @pl.loop(0, BLOCK // TALL)
+        def _(i):
+            at = rows_at(i, TALL)
+            put(down_gv, slot, i, mul(active[:, at], cot[...], TN))
+            between(j, i, 2, 3)
 
         @pl.when(j + 1 < blocks)
         def _():
             for f in fetches(j + 1, 1 - slot):
                 f.start()
 
-        @pl.loop(0, BLOCK // TALL)
-        def _(i):
-            at = rows_at(i, TALL)
-            down_gv[slot, at, :] = mul(active[:, at], cot[...], TN).astype(BF16)
-
         @pl.loop(0, width // TALL)
         def _(i):
             at = rows_at(i, TALL)
-            up_gv[slot, at, :] = mul(second[:, at], grad_hidden[...], TN).astype(BF16)
+            put(up_gv, slot, i, mul(second[:, at], grad_hidden[...], TN))
         for f in stores(j, slot):
             f.start()
-    g.at += left
+    g.at = marks[-1]
     move(attended, attended_o, 5).wait()
     output, branch = entered, attended
     gain_g[...] = jnp.zeros_like(gain_g)
@@ -616,19 +658,18 @@
     pieces = sum(len(u) for u in units_of([a.shape for a in shards]))
     anywhere, vmem = pl.BlockSpec(memory_space=pl.ANY), pl.BlockSpec(memory_space=pltpu.VMEM)
     hbm_out = [(two + a.shape, BF16) for a in shards] + [((rows, 3 * width), BF16), ((rows, width), BF16), ((rows, width), BF16),
-               ((rows, width), BF16), ((rows, width), F32), ((rows, width), BF16), ((width, ff), BF16), ((ff, width), BF16)]
+               ((rows, width), BF16), ((rows, width), F32), ((rows, width), BF16), (two + (width // owners, ff), BF16), (two + (ff // owners, width), BF16)]
     vmem_out = [((batches, pairs, length // PIECE, 2 * PIECE), F32), ((1, width), F32), ((1, ff), F32), ((1, width), F32), ((1, width), F32)]
-    lead = (ff // BLOCK).bit_length() - 1
     V = pltpu.VMEM
     return pl.pallas_call(
         functools.partial(forward_kernel, table),
         out_shape=[jax.ShapeDtypeStruct(s, d) for s, d in hbm_out + vmem_out],
-        in_specs=[vmem, anywhere, vmem] + [anywhere] * 5,
+        in_specs=[vmem, anywhere] + [vmem] * 6,
         out_specs=[anywhere] * len(hbm_out) + [vmem] * len(vmem_out),
-        scratch_shapes=[V((rows, width), BF16), V((rows, width), BF16), V((rows, 3 * width), BF16), V((rows, width), BF16), V((rows, width), F32),
+        scratch_shapes=[V(up.shape, BF16), V((rows, width), BF16), V((rows, width), BF16), V((rows, 3 * width), BF16), V((rows, width), BF16), V((rows, width), F32),
                         V((rows, width), F32), V((rows, width), F32), V((rows, BLOCK), BF16), V((rows, BLOCK), BF16),
-                        V((2,) + two + (width // owners, BLOCK), BF16), V((2,) + two[lead:] + (ff // owners, width), BF16),
-                        V((2, width, BLOCK), BF16), V((2, BLOCK, width), BF16), V(two + packed.shape, BF16), V((2, width), F32), V((1, ff), F32),
+                        V((2,) + two + (width // owners, BLOCK), BF16), V((2,) + two + (ROWS, width), BF16),
+                        V((2,) + two + (width // owners, BLOCK), BF16), V((2,) + two + (ROWS, width), BF16), V(two + packed.shape, BF16), V((2, width), F32), V((1, ff), F32),
                         V((sum(h - l for l, _, h in spans(length)), 2 * PIECE), F32),
                         pltpu.SemaphoreType.DMA((5,)), pltpu.SemaphoreType.DMA((pieces, steps)), pltpu.SemaphoreType.DMA((pieces, steps)),
                         pltpu.SemaphoreType.DMA((14,))],
@@ -733,7 +774,7 @@
 
 def scatter_chunks(table, tails):
     two = orders(table)
-    units = units_of(tails)
+    units = in_turn(units_of(tails), 0)
     return units, [piece + (two[(h + u) % 2],) for u, unit in enumerate(units) for h, piece in enumerate(unit)]
 
 
@@ -775,9 +816,9 @@
 
 def backward_kernel(table, x_hbm, start, project_hbm, attended_hbm, entered_hbm, middle_hbm, branch_hbm, qkv, out_w, up_g, down_g,
                     logsum, first_row, up_b_g, gain_g, down_b_g,
-                    grad_o, out_g, q_g, k_g, v_g, up_r, down_r, out_r, q_r, k_r, v_r, small_r,
+                    grad_o, out_g, q_g, k_g, v_g, up_o, down_r, out_r, q_r, k_r, v_r, small_r,
                     project, attended, branch, entered, weight, held, back, old, bias, k_sum, v_sum, small, stage,
-                    r0, r1, r2, r3, r4, s0, s1, s2, s3, s4, local_sem, send_sem, recv_sem, sems):
+                    up_r, r0, r1, r2, r3, r4, s0, s1, s2, s3, s4, local_sem, send_sem, recv_sem, sems):
     bits, where = my_bits(table)
     steps, owners = len(table), 2 ** len(table)
     rows, width = attended.shape
@@ -902,9 +943,11 @@
     share = width // owners
     zero = jnp.zeros((owners, 6, 128), F32)
     vectors = by_owner(first_g, 0, owners) + by_owner(gain_g[...], share, owners) + by_owner(down_b_g[...], 2 * share, owners)
-    packed = jnp.concatenate([by_owner(up_b_g[...], 0, owners)[:, None], vectors[:, None], zero], axis=1)
+    long = sum(by_owner(up_b_g[:, j * BLOCK:(j + 1) * BLOCK], j * ROWS, owners) for j in range(up_b_g.shape[1] // BLOCK))
+    packed = jnp.concatenate([long[:, None], vectors[:, None], zero], axis=1)
     small[...] = packed.reshape(small.shape)
     e.finish()
+    regroup(up_r, up_o, False)
     move(back, grad_o, 13).wait()
 
 
@@ -916,8 +959,6 @@
     length = start.shape[2]
     two = (2,) * steps
     share = width // owners
-    up_g = up_g.reshape(two + (share, up_g.shape[1]))
-    down_g = down_g.reshape(two + (down_g.shape[0] // owners, width))
     small = (8, 128)
     tails = [up_g.shape[-2:], down_g.shape[-2:]] + [(share, width)] * 4 + [small]
     units, chunks = scatter_chunks(table, tails)
@@ -935,7 +976,7 @@
                         V((2,) + two + (share, width), BF16), V((2,) + two + (share, width), BF16), V((rows, width), F32), V((2, 128, width), F32),
                         V((sum(h - l for l, _, h in spans(length)), 2 * PIECE), F32), V((length, 128), F32), V((length, 128), F32),
                         V(two + small, F32), V((4,) + two[1:] + piece, BF16)]
-        + [V((m - 1,) + two[s + 1:] + piece, BF16) for s in range(steps)] + [V(two[s + 1:] + small, F32) for s in range(steps)]
+        + [V(tails[0], F32)] + [V((m - 1,) + two[s + 1:] + piece, BF16) for s in range(steps)] + [V(two[s + 1:] + small, F32) for s in range(steps)]
         + [pltpu.SemaphoreType.DMA((4,)), pltpu.SemaphoreType.DMA((m, steps)), pltpu.SemaphoreType.DMA((m, steps)), pltpu.SemaphoreType.DMA((14,))],
         compiler_params=pltpu.CompilerParams(collective_id=collective_id, has_side_effects=True, vmem_limit_bytes=60 * 2 ** 20),
         name="backward",
@@ -949,7 +990,7 @@
 
 
 def fits(sizes, shards):
-    return all(s & (s - 1) == 0 for s in sizes.values()) and all(a.shape[0] % ROWS == 0 for a in shards)
+    return all(s & (s - 1) == 0 for s in sizes.values()) and all(a.shape[0] % ROWS == 0 for a in shards) and sizes["dp"] * sizes["fsdp"] * ROWS == BLOCK
 
 
 def item_starts(lengths, rows):

time: 362 us -> 331 us (0.914)
  Pallas kernels: 345 us -> 315 us
    pallas_call x1, Pallas kernels: 209 us -> 183 us  [forward(): pl.pallas_call(functools.partial(forward_kernel, table), out_shape=[jax.S...]
    pallas_call x1, Pallas kernels: 136 us -> 131 us  [backward(): pl.pallas_call(functools.partial(backward_kernel, table), out_shape=[jax....]
where the time goes in v4:
time: 331 us; the launch traced here: 330 us
  Pallas kernels  315 us (95%)
  local copies, waits for them, and re-layouts  10.4 us (3%)
  other arithmetic  4.7 us (1%)
    pallas_call x1, Pallas kernels, forward(): pl.pallas_call(functools.partial(forward_kernel, table), out_shape=[jax.S...  183 us
    pallas_call x1, Pallas kernels, backward(): pl.pallas_call(functools.partial(backward_kernel, table), out_shape=[jax....  131 us
    unnamed x15, local copies, waits for them, and re-layouts  7.21 us

profile of v4, /device:TPU:0, one launch (start us, length us, event | category | flops | bytes accessed | tf_op | source)
XLA Modules:
  0.0 330.3 jit_solution(14580327750505084457)
XLA Ops:
  0.6 0.8 fusion.3
  1.4 0.8 select_reduce_fusion.1
  2.2 0.1 select_reduce_fusion
  2.3 0.6 broadcast_in_dim.45.start
  2.9 1.3 fusion.2.small_s
  4.1 183.3 %forward.1 = (bf16[2,2,2,2,2,16,128]{6,5,4,3,2,1,0:T(8,128)(2,1)}, bf16[2,2,2,2,2,32,3072]{6,5,4,3,2,1,0:T(8,128)(2,1)}, bf16[2,2,2,2,2,32,1024]{6,5,4,3,2,1,0:T...) custom-call(bf16[1024,1024]{1,0:T(8,128)(2,1)} %bitcast.16, ...), custom_call_target="tpu_custom_call" | custom-call | tf_op jit(solution)/shard_map/forward/pallas_call | solution.py:664
  187.5 0.0 copy-start.1
  187.5 131.2 %backward.1 = (f32[1024,1024]{1,0:T(8,128)}, bf16[2,2,2,2,2,32,1024]{6,5,4,3,2,1,0:T(8,128)(2,1)}, bf16[2,2,2,2,2,32,1024]{6,5,4,3,2,1,0:T(8,128)(2,1)}, bf16[2,...) custom-call(bf16[1024,1024]{1,0:T(8,128)(2,1)} %bitcast.17, ...), custom_call_target="tpu_custom_call" | custom-call | tf_op jit(solution)/shard_map/backward/pallas_call | solution.py:970
  318.7 1.2 slice_bitcast_fusion.1
  319.9 1.4 slice_bitcast_fusion
  321.3 1.8 pad_maximum_fusion
  323.1 0.0 copy-done.1
  323.1 0.0 copy-start
  323.1 1.3 copy.26
  324.4 1.6 copy-done
  326.0 0.0 copy-start.4
  326.0 0.0 copy-start.3
  326.0 0.0 copy-start.2
  326.0 2.0 copy.27
  328.0 0.0 copy-done.4
  328.0 0.7 copy.28
  328.7 0.0 copy-done.3
  328.7 0.8 copy.29
  329.5 0.0 copy-done.2
  329.5 0.8 copy.30
  (1 shorter events, 0.0 us)
Async XLA Ops:
  187.5 135.6 %copy-start.1 = (bf16[1024,1024]{1,0:T(8,128)(2,1)S(1)}, bf16[1024,1024]{1,0:T(8,128)(2,1)}, u32[]{:S(2)}) copy-start(bf16[1024,1024]{1,0:T(8,128)(2,1)} %get-tuple-element.33) | copy-start | bytes 6291460
  323.1 2.9 copy-start
  326.0 2.0 copy-start.4
  326.0 2.7 copy-start.3
  326.0 3.5 %copy-start.2 = (f32[128,1024]{1,0:T(8,128)S(1)}, f32[128,1024]{1,0:T(8,128)}, u32[]{:S(2)}) copy-start(f32[128,1024]{1,0:T(8,128)} %get-tuple-element.77) | copy-start | bytes 1572868

commit v5 on v4

--- a/solution.py
+++ b/solution.py
@@ -816,7 +816,7 @@
 
 def backward_kernel(table, x_hbm, start, project_hbm, attended_hbm, entered_hbm, middle_hbm, branch_hbm, qkv, out_w, up_g, down_g,
                     logsum, first_row, up_b_g, gain_g, down_b_g,
-                    grad_o, out_g, q_g, k_g, v_g, up_o, down_r, out_r, q_r, k_r, v_r, small_r,
+                    grad_o, out_g, q_g, k_g, v_g, up_o, down_r, out_r, qkv_r, small_r,
                     project, attended, branch, entered, weight, held, back, old, bias, k_sum, v_sum, small, stage,
                     up_r, r0, r1, r2, r3, r4, s0, s1, s2, s3, s4, local_sem, send_sem, recv_sem, sems):
     bits, where = my_bits(table)
@@ -824,7 +824,7 @@
     rows, width = attended.shape
     length = start.shape[2]
     pairs = width // 128
-    e = Scatter(table, bits, where, [up_g, down_g, out_g, q_g, k_g, v_g, small], [up_r, down_r, out_r, q_r, k_r, v_r, small_r],
+    e = Scatter(table, bits, where, [up_g, down_g, out_g, q_g, k_g, v_g, small], [up_r, down_r, out_r, *[qkv_r.at[:, u * width:(u + 1) * width] for u in range(3)], small_r],
                 [r0, r1, r2, r3, r4], stage, [s0, s1, s2, s3, s4], local_sem, send_sem, recv_sem)
 
     def move(src, dst, k):
@@ -966,12 +966,12 @@
     piece = (min(ROWS, share), WIDE)
     anywhere, vmem = pl.BlockSpec(memory_space=pl.ANY), pl.BlockSpec(memory_space=pltpu.VMEM)
     V = pltpu.VMEM
-    out_shape = [((rows, width), F32)] + [(two + (share, width), BF16)] * 4 + [(t, F32) for t in tails]
+    out_shape = [((rows, width), F32)] + [(two + (share, width), BF16)] * 4 + [(t, F32) for t in (*tails[:3], (share, 3 * width), small)]
     return pl.pallas_call(
         functools.partial(backward_kernel, table),
         out_shape=[jax.ShapeDtypeStruct(s, d) for s, d in out_shape],
         in_specs=[anywhere, vmem] + [anywhere] * 9 + [vmem] * 5,
-        out_specs=[anywhere] * 5 + [vmem] * 7,
+        out_specs=[anywhere] * 5 + [vmem] * 5,
         scratch_shapes=[V((rows, 3 * width), BF16), V((rows, width), BF16), V((rows, width), BF16), V((rows, width), BF16),
                         V((2,) + two + (share, width), BF16), V((2,) + two + (share, width), BF16), V((rows, width), F32), V((2, 128, width), F32),
                         V((sum(h - l for l, _, h in spans(length)), 2 * PIECE), F32), V((length, 128), F32), V((length, 128), F32),
@@ -1047,20 +1047,21 @@
         start = item_starts(lengths[:, 0], shape[1])
         (_, qkv, out, _, _, project, attended, entered, output, middle, branch, up_g, down_g, logsum, first, up_b_g, second_g, down_b_g) = forward(
             x_val, cot, start, pack(*vectors), qkv_s, out_s, down_s, up_s, sizes, 1)
-        frames_grad, _, _, _, _, up_g, down_g, out_g, q_g, k_g, v_g, small = backward(
+        frames_grad, _, _, _, _, up_g, down_g, out_g, qkv_g, small = backward(
             x_val, start, project, attended, entered, middle, branch, qkv, out, up_g, down_g, logsum, first, up_b_g, second_g, down_b_g, sizes, 2)
         output, frames_grad = output.reshape(shape), frames_grad.reshape(shape)
         share = vectors[0].shape[0]
         first_g, second_g, down_b_g = [small[1, k * share:(k + 1) * share] for k in range(3)]
-        up_b_g, qkv_g = small[0, :vectors[2].shape[0]], [q_g, k_g, v_g]
+        up_b_g = small[0, :vectors[2].shape[0]]
     else:
         qkv, out, up, down = [lax.all_gather(w, AXES, axis=0, tiled=True) for w in weights]
         first, second, up_b, down_b = [lax.all_gather(v, AXES, axis=0, tiled=True) for v in vectors]
         params = (first, qkv, out, second, up, up_b, down, down_b)
         output, frames_grad, big, small = block_pass(frames, lengths[:, 0], cotangent, params, F32)
         down_g, up_g, out_g, *qkv_g = [lax.psum_scatter(g, AXES, scatter_dimension=0, tiled=True) for g in big]
+        qkv_g = jnp.concatenate(qkv_g, axis=1)
         first_g, second_g, up_b_g, down_b_g = [lax.psum_scatter(g, AXES, scatter_dimension=0, tiled=True) for g in small]
-    return (output, frames_grad, first_g, jnp.concatenate(qkv_g, axis=1), out_g, second_g, up_g, up_b_g, down_g, down_b_g)
+    return (output, frames_grad, first_g, qkv_g, out_g, second_g, up_g, up_b_g, down_g, down_b_g)
 
 
 def solution(mesh):

time: 331 us -> 330 us (level)
    unnamed x15 -> x18, local copies, waits for them, and re-layouts: 7.21 us -> 7.96 us
where the time goes in v5:
time: 330 us; the launch traced here: 329 us
  Pallas kernels  314 us (95%)
  local copies, waits for them, and re-layouts  11.1 us (3%)
    pallas_call x1, Pallas kernels, forward(): pl.pallas_call(functools.partial(forward_kernel, table), out_shape=[jax.S...  183 us
    pallas_call x1, Pallas kernels, backward(): pl.pallas_call(functools.partial(backward_kernel, table), out_shape=[jax....  131 us
    unnamed x18, local copies, waits for them, and re-layouts  7.96 us

profile of v5, /device:TPU:0, one launch (start us, length us, event | category | flops | bytes accessed | tf_op | source)
XLA Modules:
  0.0 329.2 jit_solution(14207333784867067371)
XLA Ops:
  0.6 0.8 fusion.3
  1.4 0.8 select_reduce_fusion.1
  2.2 0.1 select_reduce_fusion
  2.3 0.6 broadcast_in_dim.45.start
  2.9 1.3 fusion.2.small_s
  4.1 183.3 %forward.1 = (bf16[2,2,2,2,2,16,128]{6,5,4,3,2,1,0:T(8,128)(2,1)}, bf16[2,2,2,2,2,32,3072]{6,5,4,3,2,1,0:T(8,128)(2,1)}, bf16[2,2,2,2,2,32,1024]{6,5,4,3,2,1,0:T...) custom-call(bf16[1024,1024]{1,0:T(8,128)(2,1)} %bitcast.16, ...), custom_call_target="tpu_custom_call" | custom-call | tf_op jit(solution)/shard_map/forward/pallas_call | solution.py:664
  187.4 0.0 copy-start.1
  187.4 131.2 %backward.1 = (f32[1024,1024]{1,0:T(8,128)}, bf16[2,2,2,2,2,32,1024]{6,5,4,3,2,1,0:T(8,128)(2,1)}, bf16[2,2,2,2,2,32,1024]{6,5,4,3,2,1,0:T(8,128)(2,1)}, bf16[2,...) custom-call(bf16[1024,1024]{1,0:T(8,128)(2,1)} %bitcast.17, ...), custom_call_target="tpu_custom_call" | custom-call | tf_op jit(solution)/shard_map/backward/pallas_call | solution.py:970
  318.7 1.2 slice_bitcast_fusion.1
  319.8 1.4 slice_bitcast_fusion
  321.2 0.0 copy-done.1
  321.2 0.0 copy-start
  321.2 1.3 copy.27
  322.6 1.6 copy-done
  324.2 0.0 copy-start.4
  324.2 0.0 copy-start.5
  324.2 0.0 copy-start.3
  324.2 2.0 copy.28
  326.2 0.0 copy-done.4
  326.2 0.0 copy-start.2
  326.2 0.7 copy.29
  327.0 0.0 copy-done.5
  327.0 0.7 copy.30
  327.6 0.0 copy-done.3
  327.6 0.8 copy.31
  328.4 0.0 copy-done.2
  328.4 0.8 copy.32
  (1 shorter events, 0.0 us)
Async XLA Ops:
  187.4 133.8 %copy-start.1 = (bf16[1024,1024]{1,0:T(8,128)(2,1)S(1)}, bf16[1024,1024]{1,0:T(8,128)(2,1)}, u32[]{:S(2)}) copy-start(bf16[1024,1024]{1,0:T(8,128)(2,1)} %get-tuple-element.31) | copy-start | bytes 6291460
  321.2 2.9 copy-start
  324.2 2.0 copy-start.4
  324.2 2.8 copy-start.5
  324.2 3.4 %copy-start.3 = (f32[32,4096]{1,0:T(8,128)S(1)}, f32[32,4096]{1,0:T(8,128)}, u32[]{:S(2)}) copy-start(f32[32,4096]{1,0:T(8,128)} %get-tuple-element.71) | copy-start | bytes 1572868
  326.2 2.2 copy-start.2
